TPU v7x, 32 devices: a whole 2x2x4 slice. The times are simulated.
32 devices in a mesh: row: 4 (over x, core), col: 8 (over z, y).
Axes of the slice: x: 2, y: 2, z: 4, core: 2. Of those that a mesh axis runs over, the one named last changes fastest.
Arguments:
- pair: bfloat16 [8, 4, 2, 64, 128], P(None, 'row', None, 'col'), may hold values from -5 to 5
- w_query: bfloat16 [2, 2, 128, 256], replicated, may hold values from -4 to 4
- w_key: bfloat16 [2, 2, 128, 256], replicated, may hold values from -4 to 4
- w_value: bfloat16 [2, 2, 128, 256], replicated, may hold values from -0.5 to 0.5
- w_gate: bfloat16 [2, 2, 128, 256], replicated, may hold values from -0.5 to 0.5
- w_out: bfloat16 [2, 2, 256, 128], replicated, may hold values from -3 to 3
- w_in: bfloat16 [2, 128, 512], replicated, may hold values from -0.5 to 0.5
- w_back: bfloat16 [2, 512, 128], replicated, may hold values from -0.25 to 0.25
Outputs:
- pair_out: bfloat16 [8, 4, 2, 64, 128], P(None, 'row', None, 'col')
All inputs are finite; a program needn't handle non-finite values.
Results may differ from a plain program's by a relative error of at most 0.03.
Values may be sent and summed in bfloat16 or wider, within the bound.
No kernel may reach another device: no remote copies, remote signals or barrier semaphores. Data moves between devices by JAX's collectives and lax.ppermute only.
A program may use at most 64 MiB of HBM per device.

v0:
```python
import jax
import jax.numpy as jnp
from jax import lax
from jax.sharding import PartitionSpec as P

HEADS = 8
HEAD_DIM = 32


epsilon = 1e-05


def layer_norm(values):
    wide = values.astype(jnp.float32)
    center = wide - jnp.mean(wide, axis=-1, keepdims=True)
    spread = jnp.mean(center * center, axis=-1, keepdims=True)
    return (center * lax.rsqrt(spread + epsilon)).astype(jnp.bfloat16)


def split_heads(matrix):
    return matrix.reshape(matrix.shape[0], HEADS, matrix.shape[1] // HEADS)


def attend(normed, weights, direction, pattern):
    project = pattern + ",chd->ehqd"
    queries = jnp.einsum(
        project, normed, split_heads(weights[0][direction]), preferred_element_type=jnp.float32
    ).astype(jnp.bfloat16)
    key_rows = jnp.einsum(
        project, normed, split_heads(weights[1][direction]), preferred_element_type=jnp.float32
    ).astype(jnp.bfloat16)
    value_rows = jnp.einsum(
        project, normed, split_heads(weights[2][direction]), preferred_element_type=jnp.float32
    ).astype(jnp.bfloat16)
    gating = jax.nn.sigmoid(
        jnp.einsum(
            project, normed, split_heads(weights[3][direction]), preferred_element_type=jnp.float32
        )
    )
    scores = jnp.einsum(
        "ehqd,ehkd->ehqk", queries, key_rows, preferred_element_type=jnp.float32
    ) * HEAD_DIM ** (-0.5)
    maximum = jnp.max(scores, axis=-1, keepdims=True)
    exponent = jnp.exp(scores - maximum)
    denominator = jnp.sum(exponent, axis=-1, keepdims=True)
    blended = (
        jnp.einsum(
            "ehqk,ehkd->ehqd",
            exponent.astype(jnp.bfloat16),
            value_rows,
            preferred_element_type=jnp.float32,
        )
        / denominator
    )
    gated_out = (gating * blended).astype(jnp.bfloat16)
    out_matrix = weights[4][direction]
    out_heads = out_matrix.reshape(HEADS, out_matrix.shape[0] // HEADS, out_matrix.shape[1])
    return jnp.einsum(
        "ehqd,hdc->" + pattern, gated_out, out_heads, preferred_element_type=jnp.float32
    )


def local(pair, w_query, w_key, w_value, w_gate, w_out, w_in, w_back):
    row_count = lax.axis_size("row")
    col_count = lax.axis_size("col")
    span_rows = pair.shape[2]
    col_width = pair.shape[3]
    channels = pair.shape[4]
    length = col_count * col_width
    pair_tile = pair.reshape(col_count, span_rows, col_width, channels)

    def layer_step(pair_tile, layer_weights):
        attn_weights = layer_weights[:5]
        row_slab = lax.all_to_all(
            pair_tile, "col", split_axis=0, concat_axis=2, tiled=True
        ).reshape(span_rows, length, channels)
        row_update = attend(layer_norm(row_slab), attn_weights, 0, "eqc")
        row_slab = (row_slab.astype(jnp.float32) + row_update).astype(jnp.bfloat16)
        pair_tile = lax.all_to_all(
            row_slab.reshape(1, span_rows, length, channels),
            "col",
            split_axis=2,
            concat_axis=0,
            tiled=True,
        )
        pair_tile = pair_tile.reshape(col_count, span_rows, row_count, span_rows, channels)
        col_slab = lax.all_to_all(pair_tile, "row", split_axis=2, concat_axis=1, tiled=True)
        col_slab = col_slab.reshape(length, span_rows, channels)
        col_update = attend(layer_norm(col_slab), attn_weights, 1, "qec")
        col_slab = (col_slab.astype(jnp.float32) + col_update).astype(jnp.bfloat16)
        pair_tile = lax.all_to_all(
            col_slab.reshape(col_count, row_count * span_rows, 1, span_rows, channels),
            "row",
            split_axis=1,
            concat_axis=2,
            tiled=True,
        )
        pair_tile = pair_tile.reshape(col_count, span_rows, col_width, channels)
        mirrored = lax.all_to_all(
            col_slab.reshape(col_count, col_width, span_rows, channels),
            "col",
            split_axis=0,
            concat_axis=2,
            tiled=True,
        )
        mirrored = jnp.transpose(
            mirrored.reshape(col_width, col_count * span_rows, channels), (1, 0, 2)
        )
        mirrored = mirrored.reshape(col_count, span_rows, col_width, channels)
        symmetric = (0.5 * (pair_tile.astype(jnp.float32) + mirrored.astype(jnp.float32))).astype(
            jnp.bfloat16
        )
        normed = layer_norm(symmetric)
        hidden = jax.nn.relu(
            jnp.einsum(
                "aewc,cf->aewf", normed, layer_weights[5], preferred_element_type=jnp.float32
            )
        ).astype(jnp.bfloat16)
        ff_out = jnp.einsum(
            "aewf,fc->aewc", hidden, layer_weights[6], preferred_element_type=jnp.float32
        )
        pair_tile = (symmetric.astype(jnp.float32) + ff_out).astype(jnp.bfloat16)
        return (pair_tile, None)

    final_tile, unused = lax.scan(
        layer_step, pair_tile, (w_query, w_key, w_value, w_gate, w_out, w_in, w_back)
    )
    return final_tile.reshape(pair.shape)


def solution(mesh):
    return jax.shard_map(
        local,
        mesh=mesh,
        in_specs=(P(None, "row", None, "col", None), P(), P(), P(), P(), P(), P(), P()),
        out_specs=P(None, "row", None, "col", None),
        check_vma=False,
    )
```

profile of v0, /device:TPU:0, one launch (start us, length us, event | category | flops | bytes accessed | tf_op | source)
XLA Modules:
  0.0 107.8 jit_solution(3310509233860805337)
XLA Ops:
  0.0 1.4 %copy.155 = bf16[8,1,2,8,128]{4,3,2,1,0:T(8,128)(2,1)} copy(bf16[8,1,2,8,128]{4,3,2,1,0:T(8,128)(2,1)} %param.10) | data formatting | bytes 65536
  1.4 106.4 %while.10 = (s32[]{:T(128)}, bf16[8,2,8,128]{3,2,1,0:T(8,128)(2,1)}, bf16[2,2,128,256]{3,2,1,0:T(8,128)(2,1)}, bf16[2,2,128,256]{3,2,1,0:T(8,128)(2,1)}, bf16[2,...) while((s32[]{:T(128)}, ...), condition=%wide.region_11.12_spmd, body=%wide.region_0.11_spmd.sunk | while | flops 136704384 | bytes 13559725 | solution.py:125
  1.4 7.3 %all-to-all-start = ((bf16[8,2,8,128]{3,2,1,0:T(8,128)(2,1)}), bf16[8,2,8,128]{3,2,1,0:T(8,128)(2,1)S(1)}, u32[]{:S(2)}, u32[]{:S(2)}) async-start(bf16[8,2,8,128]{3,2,1,0:T(8,128)(2,1)} %get-tuple-element.218), calls=%async_computation | async-start | bytes 65536 | tf_op jit(solution)/shard_map/while/body/eval_jaxpr/all_to_all | solution.py:74
  8.7 1.0 constant_dynamic-slice_fusion.15
  9.9 0.9 copy-done
  11.3 4.1 %all-to-all-done = bf16[8,2,8,128]{3,2,1,0:T(8,128)(2,1)S(1)} async-done(((bf16[8,2,8,128]{3,2,1,0:T(8,128)(2,1)}), bf16[8,2,8,128]{3,2,1,0:T(8,128)(2,1)S(1)}, u32[]{:S(2)}, u32[]{:S(2)}) %all-to-all-start) | async-done | bytes 32800 | tf_op jit(solution)/shard_map/while/body/eval_jaxpr/all_to_all | solution.py:74
  17.6 9.1 %all_to_all.56 = bf16[1,2,64,128]{3,1,0,2:T(2,128)(2,1)S(1)} all-to-all(bf16[1,2,64,128]{3,1,0,2:T(2,128)(2,1)S(1)} %copy.137), channel_id=1, replica_groups=mesh['row'=4,'col'=8] {'col'}, dimensions={2} | all-to-all | bytes 65536 | tf_op jit(solution)/shard_map/while/body/eval_jaxpr/all_to_all | solution.py:79
  26.7 0.6 copy.138
  27.3 3.3 %all-to-all-start.2 = ((bf16[8,2,4,2,128]{4,1,0,3,2:T(2,128)(2,1)}), bf16[8,2,4,2,128]{4,1,0,3,2:T(2,128)(2,1)S(1)}, u32[]{:S(2)}, u32[]{:S(2)}) async-start(bf16[8,2,4,2,128]{4,1,0,3,2:T(2,128)(2,1)} %bitcast.387), calls=%async_computation.2 | async-start | bytes 65536 | tf_op jit(solution)/shard_map/while/body/eval_jaxpr/all_to_all | solution.py:87
  31.1 3.4 %all-to-all-done.2 = bf16[8,2,4,2,128]{4,1,0,3,2:T(2,128)(2,1)S(1)} async-done(((bf16[8,2,4,2,128]{4,1,0,3,2:T(2,128)(2,1)}), bf16[8,2,4,2,128]{4,1,0,3,2:T(2,128)(2,1)S(1)}, u32[]{:S(2)}, u32[]{:S(2)}) %all-to-all-start.2) | async-done | bytes 32800 | tf_op jit(solution)/shard_map/while/body/eval_jaxpr/all_to_all | solution.py:87
  36.9 0.6 copy.146
  37.5 3.3 %all-to-all-start.4 = ((bf16[8,8,1,2,128]{4,0,3,2,1:T(8,128)(2,1)}), bf16[8,8,1,2,128]{4,0,3,2,1:T(8,128)(2,1)S(1)}, u32[]{:S(2)}, u32[]{:S(2)}) async-start(bf16[8,8,1,2,128]{4,0,3,2,1:T(8,128)(2,1)} %copy.146), calls=%async_computation.4 | async-start | bytes 65536 | tf_op jit(solution)/shard_map/while/body/eval_jaxpr/all_to_all | solution.py:91
  40.8 0.6 copy.145
  41.4 3.3 %all-to-all-done.4 = bf16[8,8,1,2,128]{4,0,3,2,1:T(8,128)(2,1)S(1)} async-done(((bf16[8,8,1,2,128]{4,0,3,2,1:T(8,128)(2,1)}), bf16[8,8,1,2,128]{4,0,3,2,1:T(8,128)(2,1)S(1)}, u32[]{:S(2)}, u32[]{:S(2)}) %all-to-all-start.4) | async-done | bytes 32800 | tf_op jit(solution)/shard_map/while/body/eval_jaxpr/all_to_all | solution.py:91
  44.7 3.3 %all-to-all-start.3 = ((bf16[8,8,2,128]{3,1,2,0:T(8,128)(2,1)}), bf16[8,8,2,128]{3,1,2,0:T(8,128)(2,1)S(1)}, u32[]{:S(2)}, u32[]{:S(2)}) async-start(bf16[8,8,2,128]{3,1,2,0:T(8,128)(2,1)} %copy.145), calls=%async_computation.3 | async-start | bytes 65536 | tf_op jit(solution)/shard_map/while/body/eval_jaxpr/all_to_all | solution.py:99
  48.1 6.6 %all-to-all-done.3 = bf16[8,8,2,128]{3,1,2,0:T(8,128)(2,1)S(1)} async-done(((bf16[8,8,2,128]{3,1,2,0:T(8,128)(2,1)}), bf16[8,8,2,128]{3,1,2,0:T(8,128)(2,1)S(1)}, u32[]{:S(2)}, u32[]{:S(2)}) %all-to-all-start.3) | async-done | bytes 32800 | tf_op jit(solution)/shard_map/while/body/eval_jaxpr/all_to_all | solution.py:99
  55.7 0.9 fusion.195
  56.6 3.3 %all-to-all-start = ((bf16[8,2,8,128]{3,2,1,0:T(8,128)(2,1)}), bf16[8,2,8,128]{3,2,1,0:T(8,128)(2,1)S(1)}, u32[]{:S(2)}, u32[]{:S(2)}) async-start(bf16[8,2,8,128]{3,2,1,0:T(8,128)(2,1)} %get-tuple-element.218), calls=%async_computation | async-start | bytes 65536 | tf_op jit(solution)/shard_map/while/body/eval_jaxpr/all_to_all | solution.py:74
  60.0 1.0 constant_dynamic-slice_fusion.15
  61.1 0.9 copy-done
  62.6 4.0 %all-to-all-done = bf16[8,2,8,128]{3,2,1,0:T(8,128)(2,1)S(1)} async-done(((bf16[8,2,8,128]{3,2,1,0:T(8,128)(2,1)}), bf16[8,2,8,128]{3,2,1,0:T(8,128)(2,1)S(1)}, u32[]{:S(2)}, u32[]{:S(2)}) %all-to-all-start) | async-done | bytes 32800 | tf_op jit(solution)/shard_map/while/body/eval_jaxpr/all_to_all | solution.py:74
  68.8 9.1 %all_to_all.56 = bf16[1,2,64,128]{3,1,0,2:T(2,128)(2,1)S(1)} all-to-all(bf16[1,2,64,128]{3,1,0,2:T(2,128)(2,1)S(1)} %copy.137), channel_id=1, replica_groups=mesh['row'=4,'col'=8] {'col'}, dimensions={2} | all-to-all | bytes 65536 | tf_op jit(solution)/shard_map/while/body/eval_jaxpr/all_to_all | solution.py:79
  77.9 0.6 copy.138
  78.5 3.3 %all-to-all-start.2 = ((bf16[8,2,4,2,128]{4,1,0,3,2:T(2,128)(2,1)}), bf16[8,2,4,2,128]{4,1,0,3,2:T(2,128)(2,1)S(1)}, u32[]{:S(2)}, u32[]{:S(2)}) async-start(bf16[8,2,4,2,128]{4,1,0,3,2:T(2,128)(2,1)} %bitcast.387), calls=%async_computation.2 | async-start | bytes 65536 | tf_op jit(solution)/shard_map/while/body/eval_jaxpr/all_to_all | solution.py:87
  82.3 3.4 %all-to-all-done.2 = bf16[8,2,4,2,128]{4,1,0,3,2:T(2,128)(2,1)S(1)} async-done(((bf16[8,2,4,2,128]{4,1,0,3,2:T(2,128)(2,1)}), bf16[8,2,4,2,128]{4,1,0,3,2:T(2,128)(2,1)S(1)}, u32[]{:S(2)}, u32[]{:S(2)}) %all-to-all-start.2) | async-done | bytes 32800 | tf_op jit(solution)/shard_map/while/body/eval_jaxpr/all_to_all | solution.py:87
  88.1 0.6 copy.146
  88.7 3.3 %all-to-all-start.4 = ((bf16[8,8,1,2,128]{4,0,3,2,1:T(8,128)(2,1)}), bf16[8,8,1,2,128]{4,0,3,2,1:T(8,128)(2,1)S(1)}, u32[]{:S(2)}, u32[]{:S(2)}) async-start(bf16[8,8,1,2,128]{4,0,3,2,1:T(8,128)(2,1)} %copy.146), calls=%async_computation.4 | async-start | bytes 65536 | tf_op jit(solution)/shard_map/while/body/eval_jaxpr/all_to_all | solution.py:91
  92.0 0.6 copy.145
  92.6 3.3 %all-to-all-done.4 = bf16[8,8,1,2,128]{4,0,3,2,1:T(8,128)(2,1)S(1)} async-done(((bf16[8,8,1,2,128]{4,0,3,2,1:T(8,128)(2,1)}), bf16[8,8,1,2,128]{4,0,3,2,1:T(8,128)(2,1)S(1)}, u32[]{:S(2)}, u32[]{:S(2)}) %all-to-all-start.4) | async-done | bytes 32800 | tf_op jit(solution)/shard_map/while/body/eval_jaxpr/all_to_all | solution.py:91
  95.9 3.3 %all-to-all-start.3 = ((bf16[8,8,2,128]{3,1,2,0:T(8,128)(2,1)}), bf16[8,8,2,128]{3,1,2,0:T(8,128)(2,1)S(1)}, u32[]{:S(2)}, u32[]{:S(2)}) async-start(bf16[8,8,2,128]{3,1,2,0:T(8,128)(2,1)} %copy.145), calls=%async_computation.3 | async-start | bytes 65536 | tf_op jit(solution)/shard_map/while/body/eval_jaxpr/all_to_all | solution.py:99
  99.3 6.6 %all-to-all-done.3 = bf16[8,8,2,128]{3,1,2,0:T(8,128)(2,1)S(1)} async-done(((bf16[8,8,2,128]{3,1,2,0:T(8,128)(2,1)}), bf16[8,8,2,128]{3,1,2,0:T(8,128)(2,1)S(1)}, u32[]{:S(2)}, u32[]{:S(2)}) %all-to-all-start.3) | async-done | bytes 32800 | tf_op jit(solution)/shard_map/while/body/eval_jaxpr/all_to_all | solution.py:99
  106.9 0.9 fusion.195
  (104 shorter events, 13.1 us)
Async XLA Ops:
  1.4 14.0 %all-to-all-start = ((bf16[8,2,8,128]{3,2,1,0:T(8,128)(2,1)}), bf16[8,2,8,128]{3,2,1,0:T(8,128)(2,1)S(1)}, u32[]{:S(2)}, u32[]{:S(2)}) async-start(bf16[8,2,8,128]{3,2,1,0:T(8,128)(2,1)} %get-tuple-element.218), calls=%async_computation | async-start | bytes 65536 | tf_op jit(solution)/shard_map/while/body/eval_jaxpr/all_to_all | solution.py:74
  8.7 1.0 copy-start.3
  8.7 1.1 %copy-start.4 = (bf16[2,2,128,256]{3,2,1,0:T(8,128)(2,1)S(1)}, bf16[2,2,128,256]{3,2,1,0:T(8,128)(2,1)}, u32[]{:S(2)}) copy-start(bf16[2,2,128,256]{3,2,1,0:T(8,128)(2,1)} %get-tuple-element.232) | copy-start | bytes 786436 | tf_op jit(solution)/shard_map/while
  9.8 0.9 copy-start
  27.3 7.2 %all-to-all-start.2 = ((bf16[8,2,4,2,128]{4,1,0,3,2:T(2,128)(2,1)}), bf16[8,2,4,2,128]{4,1,0,3,2:T(2,128)(2,1)S(1)}, u32[]{:S(2)}, u32[]{:S(2)}) async-start(bf16[8,2,4,2,128]{4,1,0,3,2:T(2,128)(2,1)} %bitcast.387), calls=%async_computation.2 | async-start | bytes 65536 | tf_op jit(solution)/shard_map/while/body/eval_jaxpr/all_to_all | solution.py:87
  37.5 7.2 %all-to-all-start.4 = ((bf16[8,8,1,2,128]{4,0,3,2,1:T(8,128)(2,1)}), bf16[8,8,1,2,128]{4,0,3,2,1:T(8,128)(2,1)S(1)}, u32[]{:S(2)}, u32[]{:S(2)}) async-start(bf16[8,8,1,2,128]{4,0,3,2,1:T(8,128)(2,1)} %copy.146), calls=%async_computation.4 | async-start | bytes 65536 | tf_op jit(solution)/shard_map/while/body/eval_jaxpr/all_to_all | solution.py:91
  44.7 10.0 %all-to-all-start.3 = ((bf16[8,8,2,128]{3,1,2,0:T(8,128)(2,1)}), bf16[8,8,2,128]{3,1,2,0:T(8,128)(2,1)S(1)}, u32[]{:S(2)}, u32[]{:S(2)}) async-start(bf16[8,8,2,128]{3,1,2,0:T(8,128)(2,1)} %copy.145), calls=%async_computation.3 | async-start | bytes 65536 | tf_op jit(solution)/shard_map/while/body/eval_jaxpr/all_to_all | solution.py:99
  54.7 1.0 copy-start.1
  54.7 1.0 copy-start.2
  56.6 10.0 %all-to-all-start = ((bf16[8,2,8,128]{3,2,1,0:T(8,128)(2,1)}), bf16[8,2,8,128]{3,2,1,0:T(8,128)(2,1)S(1)}, u32[]{:S(2)}, u32[]{:S(2)}) async-start(bf16[8,2,8,128]{3,2,1,0:T(8,128)(2,1)} %get-tuple-element.218), calls=%async_computation | async-start | bytes 65536 | tf_op jit(solution)/shard_map/while/body/eval_jaxpr/all_to_all | solution.py:74
  59.9 1.0 copy-start.3
  60.0 1.1 %copy-start.4 = (bf16[2,2,128,256]{3,2,1,0:T(8,128)(2,1)S(1)}, bf16[2,2,128,256]{3,2,1,0:T(8,128)(2,1)}, u32[]{:S(2)}) copy-start(bf16[2,2,128,256]{3,2,1,0:T(8,128)(2,1)} %get-tuple-element.232) | copy-start | bytes 786436 | tf_op jit(solution)/shard_map/while
  61.1 0.9 copy-start
  78.5 7.2 %all-to-all-start.2 = ((bf16[8,2,4,2,128]{4,1,0,3,2:T(2,128)(2,1)}), bf16[8,2,4,2,128]{4,1,0,3,2:T(2,128)(2,1)S(1)}, u32[]{:S(2)}, u32[]{:S(2)}) async-start(bf16[8,2,4,2,128]{4,1,0,3,2:T(2,128)(2,1)} %bitcast.387), calls=%async_computation.2 | async-start | bytes 65536 | tf_op jit(solution)/shard_map/while/body/eval_jaxpr/all_to_all | solution.py:87
  88.7 7.2 %all-to-all-start.4 = ((bf16[8,8,1,2,128]{4,0,3,2,1:T(8,128)(2,1)}), bf16[8,8,1,2,128]{4,0,3,2,1:T(8,128)(2,1)S(1)}, u32[]{:S(2)}, u32[]{:S(2)}) async-start(bf16[8,8,1,2,128]{4,0,3,2,1:T(8,128)(2,1)} %copy.146), calls=%async_computation.4 | async-start | bytes 65536 | tf_op jit(solution)/shard_map/while/body/eval_jaxpr/all_to_all | solution.py:91
  95.9 10.0 %all-to-all-start.3 = ((bf16[8,8,2,128]{3,1,2,0:T(8,128)(2,1)}), bf16[8,8,2,128]{3,1,2,0:T(8,128)(2,1)S(1)}, u32[]{:S(2)}, u32[]{:S(2)}) async-start(bf16[8,8,2,128]{3,1,2,0:T(8,128)(2,1)} %copy.145), calls=%async_computation.3 | async-start | bytes 65536 | tf_op jit(solution)/shard_map/while/body/eval_jaxpr/all_to_all | solution.py:99
  105.8 1.0 copy-start.1
  105.9 1.0 copy-start.2
where the time goes:
time: 109 us; the launch traced here: 108 us
  waiting for transfers between devices  34.7 us (32%)
  starting transfers between devices  30.4 us (28%)
  blocking collectives  18.1 us (17%)
  local copies, waits for them, and re-layouts  12 us (11%)
  matrix products  8.3 us (8%)
  other arithmetic  3.69 us (3%)
    all_to_all x2, blocking collectives, layer_step(): lax.all_to_all(row_slab.reshape(1, span_rows, length, channels), 'col', s...  18.1 us
    all_to_all x2, waiting for transfers between devices, layer_step(): lax.all_to_all(col_slab.reshape(col_count, col_width, span_rows, channels...  13.1 us
    all_to_all x2, starting transfers between devices, layer_step(): lax.all_to_all(pair_tile, 'col', split_axis=0, concat_axis=2, tiled=True)  10.7 us
    all_to_all x2, waiting for transfers between devices, layer_step(): lax.all_to_all(pair_tile, 'col', split_axis=0, concat_axis=2, tiled=True)  8.1 us
    all_to_all x2, waiting for transfers between devices, layer_step(): lax.all_to_all(pair_tile, 'row', split_axis=2, concat_axis=1, tiled=True)  6.85 us
    all_to_all x2, starting transfers between devices, layer_step(): lax.all_to_all(col_slab.reshape(col_count, col_width, span_rows, channels...  6.68 us
    all_to_all x2, waiting for transfers between devices, layer_step(): lax.all_to_all(col_slab.reshape(col_count, row_count * span_rows, 1, span...  6.58 us
    all_to_all x2, starting transfers between devices, layer_step(): lax.all_to_all(pair_tile, 'row', split_axis=2, concat_axis=1, tiled=True)  6.53 us
  transfers between devices with their start and end apart: 8, of which 8 were waited for; matrix products, arithmetic and copies ran while one was open for 5% of the time, Pallas kernels for 0%

commit v1 on v0

--- a/solution.py
+++ b/solution.py
@@ -1,10 +1,17 @@
+import functools
+import math
+
 import jax
 import jax.numpy as jnp
 from jax import lax
+from jax.experimental import pallas as pl
+from jax.experimental.pallas import tpu as pltpu
 from jax.sharding import PartitionSpec as P
 
 HEADS = 8
 HEAD_DIM = 32
+LANES = 128
+VMEM_BUDGET = 24 * 2**20
 
 
 epsilon = 1e-05
@@ -60,7 +67,7 @@
     )
 
 
-def local(pair, w_query, w_key, w_value, w_gate, w_out, w_in, w_back):
+def local_slabs(pair, w_query, w_key, w_value, w_gate, w_out, w_in, w_back):
     row_count = lax.axis_size("row")
     col_count = lax.axis_size("col")
     span_rows = pair.shape[2]
@@ -128,11 +135,441 @@
     return final_tile.reshape(pair.shape)
 
 
+def dot(left, right, contract=((1,), (0,))):
+    return lax.dot_general(left, right, (contract, ((), ())), preferred_element_type=jnp.float32)
+
+
+NT = ((1,), (1,))
+TN = ((0,), (0,))
+
+
+def project(normed, span, weights, stores):
+    w_query, w_key, w_value_gate = weights
+    queries, keys, values, gates = stores
+    inner = w_query.shape[1]
+    queries[span, :] = dot(normed, w_query[...]).astype(jnp.bfloat16)
+    keys[span, :] = dot(normed, w_key[...]).astype(jnp.bfloat16)
+    values[:, span] = dot(w_value_gate[:inner, :], normed, NT).astype(jnp.bfloat16)
+    gates[:, span] = jax.nn.sigmoid(dot(w_value_gate[inner:, :], normed, NT))
+
+
+def attend_pair(start, length, stores, w_out):
+    queries, keys, values, gates = stores
+    both = pl.ds(start, 2 * length)
+    per_group = LANES // HEAD_DIM
+    groups = HEADS // per_group
+    scale = HEAD_DIM ** (-0.5) * math.log2(math.e)
+    lane = lax.broadcasted_iota(jnp.int32, (1, LANES), 1)
+    head_masks = [
+        (lane // HEAD_DIM == h).astype(jnp.float32).astype(jnp.bfloat16) for h in range(per_group)
+    ]
+    low = lane < length
+    low_mask = low.astype(jnp.float32).astype(jnp.bfloat16)
+    high_mask = (~low).astype(jnp.float32).astype(jnp.bfloat16)
+    gated = [None] * HEADS
+    for group in range(groups):
+        channels = slice(group * LANES, (group + 1) * LANES)
+        probs, denominators = [], []
+        for which in range(2):
+            rows = pl.ds(start + which * length, length)
+            query = queries[rows, channels]
+            order = [h ^ which for h in range(per_group)]
+            spread = jnp.concatenate([query * head_masks[h] for h in order], axis=0)
+            scores = dot(keys[rows, channels], spread, NT)
+            exponent = jnp.exp2((scores - jnp.max(scores, axis=0, keepdims=True)) * scale)
+            denominators.append(jnp.sum(exponent, axis=0, keepdims=True))
+            probs.append(exponent.astype(jnp.bfloat16))
+        for tile in range(per_group // 2):
+            columns = slice(tile * LANES, (tile + 1) * LANES)
+            first, second = probs[0][:, columns], probs[1][:, columns]
+            spread = jnp.concatenate(
+                [
+                    jnp.concatenate([first * low_mask, second * high_mask], axis=0),
+                    jnp.concatenate([first * high_mask, second * low_mask], axis=0),
+                ],
+                axis=1,
+            )
+            head = group * per_group + 2 * tile
+            inner = slice(head * HEAD_DIM, (head + 2) * HEAD_DIM)
+            blended = dot(values[inner, both], spread)
+            one, two = denominators[0][:, columns], denominators[1][:, columns]
+            even = blended[:HEAD_DIM, :LANES] / jnp.where(low, one, two)
+            odd = blended[HEAD_DIM:, LANES:] / jnp.where(low, two, one)
+            odd = pltpu.roll(odd, length, 1)
+            gate = gates[inner, both]
+            gated[head] = (gate[:HEAD_DIM] * even).astype(jnp.bfloat16)
+            gated[head + 1] = (gate[HEAD_DIM:] * odd).astype(jnp.bfloat16)
+    return dot(jnp.concatenate(gated, axis=0), w_out[...], TN)
+
+
+def rounded(values):
+    return values.astype(jnp.bfloat16).astype(jnp.float32)
+
+
+def attend_slab(grid, length, stores, w_out, unroll):
+    pair = 2 * length
+
+    def step(index, carry):
+        start = pl.multiple_of(index * pair, pair)
+        update = attend_pair(start, length, stores, w_out)
+        here = pl.ds(start, pair)
+        grid[here, :] = rounded(grid[here, :] + update)
+        return carry
+
+    lax.fori_loop(0, grid.shape[0] // pair, step, 0, unroll=unroll)
+
+
+def transition(values, w_in, w_back):
+    hidden = jnp.maximum(dot(layer_norm(values), w_in[...]), 0.0).astype(jnp.bfloat16)
+    return rounded(values + dot(hidden, w_back[...]))
+
+
+def first_row_kernel(dims, *refs):
+    blocks, pairs, span, width = dims
+    parts = refs[:4]
+    w_query, w_key, w_value_gate, w_out, keep, send, grid = refs[4:11]
+    stores = refs[11:15]
+    row, col = lax.axis_index("row"), lax.axis_index("col")
+    x, core = row // 2, row % 2
+    length = blocks * width
+    half = blocks * pairs * span
+    for number, part in enumerate(parts):
+        dx, dy = number // 2, number % 2
+        at_x = x ^ dx
+        for other in range(blocks // 2):
+            at_c = col ^ (2 * other + dy)
+            for a in range(blocks):
+                for e in range(span):
+                    at = ((a * pairs + at_x) * span + e) * length + at_c * width
+                    grid[pl.ds(pl.multiple_of(at, width), width), :] = part[other, a, e].astype(
+                        jnp.float32
+                    )
+    chunk = 4 * length
+
+    def step(index, carry):
+        here = pl.ds(pl.multiple_of(index * chunk, chunk), chunk)
+        project(layer_norm(grid[here, :]), here, (w_query, w_key, w_value_gate), stores)
+        return carry
+
+    lax.fori_loop(0, grid.shape[0] // chunk, step, 0)
+    attend_slab(grid, length, stores, w_out, 2)
+    for target, parity in ((keep, core), (send, 1 - core)):
+        for a in range(blocks):
+            for other in range(pairs):
+                for e in range(span):
+                    at = a * width + other * 2 * span + parity * span + e
+                    target[(a * pairs + other) * span + e] = grid[
+                        pl.ds(at, half, stride=length), :
+                    ].astype(jnp.bfloat16)
+
+
+def col_kernel(keep, recv, w_query, w_key, w_value_gate, w_out, slab, own, send, grid, *stores):
+    half = keep.shape[1]
+    length = 2 * half
+    count = 4
+
+    def step(index, carry):
+        seqs = pl.ds(index * count, count)
+        values = jnp.concatenate([keep[seqs], recv[seqs]], axis=1).astype(jnp.float32)
+        values = values.reshape(count * length, values.shape[2])
+        here = pl.ds(pl.multiple_of(index * count * length, count * length), count * length)
+        grid[here, :] = values
+        project(layer_norm(values), here, (w_query, w_key, w_value_gate), stores)
+        return carry
+
+    lax.fori_loop(0, half // count, step, 0)
+    attend_slab(grid, length, stores, w_out, 2)
+    for j in range(half):
+        slab[j] = grid[j * length : (j + 1) * length, :].astype(jnp.bfloat16)
+    for i in range(half):
+        own[i] = grid[pl.ds(i, half, stride=length), :].astype(jnp.bfloat16)
+        send[i] = grid[pl.ds(half + i, half, stride=length), :].astype(jnp.bfloat16)
+
+
+def mid_row_kernel(
+    dims, slab, own, recv, w_in, w_back, w_query, w_key, w_value_gate, w_out, keep, send, grid, *stores
+):
+    blocks, pairs, span, width = dims
+    half = own.shape[0]
+    length = 2 * half
+    count = 4
+    row, col = lax.axis_index("row"), lax.axis_index("col")
+    x, core = row // 2, row % 2
+
+    def step(index, carry):
+        seqs = pl.ds(index * count, count)
+        direct = jnp.concatenate([own[seqs], recv[seqs]], axis=1).astype(jnp.float32)
+        values = rounded(0.5 * (direct + slab[seqs].astype(jnp.float32)))
+        values = transition(values.reshape(count * length, values.shape[2]), w_in, w_back)
+        here = pl.ds(pl.multiple_of(index * count * length, count * length), count * length)
+        grid[here, :] = values
+        project(layer_norm(values), here, (w_query, w_key, w_value_gate), stores)
+        return carry
+
+    lax.fori_loop(0, half // count, step, 0)
+    attend_slab(grid, length, stores, w_out, 2)
+    for other in range(pairs):
+        for k in range(2):
+            for e in range(span):
+                number = (other * 2 + k) * span + e
+                inside = (col * pairs + other) * span + e
+                for target, mine in ((keep, core), (send, 1 - core)):
+                    at = inside + half * (k ^ mine)
+                    if target is send:
+                        at = inside + half * (k ^ core)
+                    else:
+                        at = inside + half * (k ^ core)
+                    target[number] = grid[pl.ds(at, half, stride=length), :].astype(jnp.bfloat16)
+    for a in range(blocks):
+        for e in range(span):
+            inside = (a * pairs + x) * span + e
+            number = width + a * span + e
+            keep[number] = grid[pl.ds(inside, half, stride=length), :].astype(jnp.bfloat16)
+            send[number] = grid[pl.ds(half + inside, half, stride=length), :].astype(jnp.bfloat16)
+
+
+def few_queries(query, keys, values, head_masks, tile_masks):
+    scale = HEAD_DIM ** (-0.5) * math.log2(math.e)
+    count = query.shape[0]
+    spread = jnp.concatenate([query * mask for mask in head_masks], axis=0)
+    scores = dot(spread, keys, NT)
+    exponent = jnp.exp2((scores - jnp.max(scores, axis=1, keepdims=True)) * scale)
+    denominator = jnp.sum(exponent, axis=1, keepdims=True)
+    blended = dot(exponent.astype(jnp.bfloat16), values) / denominator
+    total = None
+    for h in range(HEADS):
+        term = blended[h * count : (h + 1) * count] * tile_masks[h]
+        total = term if total is None else total + term
+    return total
+
+
+def last_kernel(
+    dims, keep, recv, w_query, w_key, w_value, w_gate, w_out, w_in, w_back, out, grid, keys, values, picked, blended
+):
+    blocks, pairs, span, width = dims
+    half = keep.shape[1]
+    length = 2 * half
+    seqs = keep.shape[0]
+    row, col = lax.axis_index("row"), lax.axis_index("col")
+    x, core = row // 2, row % 2
+    tall = blocks * span
+    tile = width * tall
+    chunk = 8
+    for index in range(seqs // chunk):
+        part = slice(index * chunk, (index + 1) * chunk)
+        wide = jnp.concatenate([keep[part], recv[part]], axis=1).astype(jnp.float32)
+        wide = wide.reshape(chunk * length, wide.shape[2])
+        here = slice(index * chunk * length, (index + 1) * chunk * length)
+        grid[here, :] = wide
+        normed = layer_norm(wide)
+        keys[here, :] = dot(normed, w_key[...]).astype(jnp.bfloat16)
+        values[here, :] = dot(normed, w_value[...]).astype(jnp.bfloat16)
+    for w in range(width):
+        for e in range(span):
+            at = w * length + x * span + e
+            picked[pl.ds((w * span + e) * blocks, blocks), :] = grid[
+                pl.ds(at, blocks, stride=pairs * span), :
+            ]
+    for a in range(blocks):
+        for e in range(span):
+            seq = width + a * span + e
+            for other in range(pairs):
+                for k in range(2):
+                    for e2 in range(span):
+                        w = (other * 2 + k) * span + e2
+                        at = seq * length + half * (k ^ core) + (col * pairs + other) * span + e2
+                        picked[pl.ds(tile + (e * blocks + a) * width + w, 1), :] = grid[
+                            pl.ds(at, 1), :
+                        ]
+    here = picked[...]
+    normed = layer_norm(here)
+    queries = dot(normed, w_query[...]).astype(jnp.bfloat16)
+    gating = jax.nn.sigmoid(dot(normed, w_gate[...]))
+    inner = queries.shape[1]
+    lane = lax.broadcasted_iota(jnp.int32, (1, inner), 1)
+    tile_masks = [(lane // HEAD_DIM == h).astype(jnp.float32) for h in range(HEADS)]
+    head_masks = [mask.astype(jnp.bfloat16) for mask in tile_masks]
+    for w in range(width):
+        rows = slice(w * tall, (w + 1) * tall)
+        at = slice(w * length, (w + 1) * length)
+        blended[rows, :] = few_queries(queries[rows], keys[at, :], values[at, :], head_masks, tile_masks)
+    for a in range(blocks):
+        for e in range(span):
+            start = tile + (e * blocks + a) * width
+            seq = width + a * span + e
+            rows = slice(start, start + width)
+            at = slice(seq * length, (seq + 1) * length)
+            blended[rows, :] = few_queries(
+                queries[rows], keys[at, :], values[at, :], head_masks, tile_masks
+            )
+    gated = (gating * blended[...]).astype(jnp.bfloat16)
+    picked[...] = rounded(here + dot(gated, w_out[...]))
+    for e in range(span):
+        for a in range(blocks):
+            start = (e * blocks + a) * width
+            direct = picked[pl.ds(e * blocks + a, width, stride=tall), :]
+            mirrored = picked[tile + start : tile + start + width, :]
+            grid[start : start + width, :] = rounded(0.5 * (direct + mirrored))
+    result = transition(grid[:tile, :], w_in, w_back)
+    for e in range(span):
+        for a in range(blocks):
+            start = (e * blocks + a) * width
+            out[a, 0, e] = result[start : start + width].astype(jnp.bfloat16)
+
+
+def whole(shape):
+    return pl.BlockSpec(shape, lambda i: (0,) * len(shape))
+
+
+def part_of(array, layer, direction=None):
+    lead = (layer,) if direction is None else (layer, direction)
+    shape = (None,) * len(lead) + array.shape[len(lead) :]
+    return pl.BlockSpec(shape, lambda i: lead + (0, 0))
+
+
+def call(kernel, arrays, weights, outs, scratch):
+    return pl.pallas_call(
+        kernel,
+        grid=(1,),
+        in_specs=[whole(array.shape) for array in arrays] + [part_of(*entry) for entry in weights],
+        out_specs=[whole(shape) for shape in outs],
+        out_shape=[jax.ShapeDtypeStruct(shape, jnp.bfloat16) for shape in outs],
+        scratch_shapes=scratch,
+    )(*arrays, *[entry[0] for entry in weights])
+
+
+def local_gathered(pair, w_query, w_key, w_value, w_gate, w_out, w_in, w_back):
+    row_count = lax.axis_size("row")
+    col_count = lax.axis_size("col")
+    blocks, unused, span, width, channels = pair.shape
+    inner = w_query.shape[3]
+    pairs = row_count // 2
+    length = blocks * width
+    half = length // 2
+    positions = half * length
+    dims = (blocks, pairs, span, width)
+    tile = pair.reshape(blocks, span, width, channels)
+    w_value_gate = jnp.swapaxes(jnp.concatenate([w_value, w_gate], axis=3), 2, 3)
+
+    def moved(array, dx, dc):
+        if dx == 0:
+            return lax.ppermute(array, "col", [(c, c ^ dc) for c in range(col_count)])
+        if dc == 0:
+            return lax.ppermute(array, "row", [(r, r ^ (2 * dx)) for r in range(row_count)])
+        routes = []
+        for r in range(row_count):
+            for c in range(col_count):
+                routes.append((r * col_count + c, (r ^ (2 * dx)) * col_count + (c ^ dc)))
+        return lax.ppermute(array, ("row", "col"), routes)
+
+    def to_partner(array):
+        return lax.ppermute(array, "row", [(r, r ^ 1) for r in range(row_count)])
+
+    near = jnp.stack([tile] + [moved(tile, 0, 2 * k) for k in range(1, blocks // 2)])
+    parts = []
+    for dx in range(pairs):
+        for dy in range(2):
+            parts.append(near if dx == dy == 0 else moved(near, dx, dy))
+
+    f32, bf16 = jnp.float32, jnp.bfloat16
+    grid = pltpu.VMEM((positions, channels), f32)
+    stores = [
+        pltpu.VMEM((positions, inner), bf16),
+        pltpu.VMEM((positions, inner), bf16),
+        pltpu.VMEM((inner, positions), bf16),
+        pltpu.VMEM((inner, positions), f32),
+    ]
+
+    def attention(layer, direction):
+        return [
+            (w_query, layer, direction),
+            (w_key, layer, direction),
+            (w_value_gate, layer, direction),
+            (w_out, layer, direction),
+        ]
+
+    quadrant = (half, half, channels)
+    keep, send = call(
+        functools.partial(first_row_kernel, dims),
+        parts,
+        attention(0, 0),
+        [quadrant, quadrant],
+        [grid] + stores,
+    )
+    layers = w_in.shape[0]
+    for layer in range(layers - 1):
+        slab, own, send = call(
+            col_kernel,
+            [keep, to_partner(send)],
+            attention(layer, 1),
+            [(half, length, channels), quadrant, quadrant],
+            [grid] + stores,
+        )
+        last = layer == layers - 2
+        few = (width + blocks * span, half, channels)
+        keep, send = call(
+            functools.partial(mid_row_kernel, dims),
+            [slab, own, to_partner(send)],
+            [(w_in, layer), (w_back, layer)] + attention(layer + 1, 0),
+            [few, few],
+            [grid] + stores,
+        )
+    layer = layers - 1
+    seqs = width + blocks * span
+    (result,) = call(
+        functools.partial(last_kernel, dims),
+        [keep, to_partner(send)],
+        [
+            (w_query, layer, 1),
+            (w_key, layer, 1),
+            (w_value, layer, 1),
+            (w_gate, layer, 1),
+            (w_out, layer, 1),
+            (w_in, layer),
+            (w_back, layer),
+        ],
+        [pair.shape],
+        [
+            pltpu.VMEM((seqs * length, channels), f32),
+            pltpu.VMEM((seqs * length, inner), bf16),
+            pltpu.VMEM((seqs * length, inner), bf16),
+            pltpu.VMEM((2 * width * blocks * span, channels), f32),
+            pltpu.VMEM((2 * width * blocks * span, inner), f32),
+        ],
+    )
+    return result
+
+
+def fits_gathered(mesh, pair, w_query, w_in):
+    row_count, col_count = mesh.shape["row"], mesh.shape["col"]
+    blocks, groups, span, total, channels = pair.shape
+    width = total // col_count
+    length = blocks * groups * span
+    inner = w_query.shape[3]
+    sizes_ok = (
+        groups == row_count == 4
+        and blocks == col_count
+        and col_count & (col_count - 1) == 0
+        and width == 8
+        and 2 * length == LANES
+        and channels == LANES
+        and inner == HEADS * HEAD_DIM
+        and w_in.shape[0] == 2
+    )
+    half = length * length // 2
+    return sizes_ok and half * (4 * channels + 10 * inner) < VMEM_BUDGET
+
+
 def solution(mesh):
-    return jax.shard_map(
-        local,
-        mesh=mesh,
-        in_specs=(P(None, "row", None, "col", None), P(), P(), P(), P(), P(), P(), P()),
-        out_specs=P(None, "row", None, "col", None),
-        check_vma=False,
-    )
+    def run(*arrays):
+        pair, w_query, w_in = arrays[0], arrays[1], arrays[6]
+        body = local_gathered if fits_gathered(mesh, pair, w_query, w_in) else local_slabs
+        return jax.shard_map(
+            body,
+            mesh=mesh,
+            in_specs=(P(None, "row", None, "col", None), P(), P(), P(), P(), P(), P(), P()),
+            out_specs=P(None, "row", None, "col", None),
+            check_vma=False,
+        )(*arrays)
+
+    return run

time: 109 us -> 90.9 us (0.83)
  Pallas kernels: 0 us -> 63.5 us
  waiting for transfers between devices: 34.7 us -> 12.5 us
  starting transfers between devices: 30.4 us -> 9.54 us
  blocking collectives: 18.1 us -> 0 us
  local copies, waits for them, and re-layouts: 12 us -> 3.36 us
  matrix products: 8.3 us -> 0 us
  other arithmetic: 3.69 us -> 1.61 us
    pallas_call x0 -> x4, Pallas kernels: none -> 63.5 us  [call(): pl.pallas_call(kernel, grid=(1,), in_specs=[whole(array.shape) for array...]
    all_to_all x8 -> x0, waiting for transfers between devices: 34.7 us -> none  [the longest x2 13.1 us: layer_step(): lax.all_to_all(col_slab.reshape(col_count, col_width, span_rows, channels...]
    all_to_all x8 -> x0, starting transfers between devices: 30.4 us -> none  [the longest x2 10.7 us: layer_step(): lax.all_to_all(pair_tile, 'col', split_axis=0, concat_axis=2, tiled=True)]
    all_to_all x2 -> x0, blocking collectives: 18.1 us -> none  [layer_step(): lax.all_to_all(row_slab.reshape(1, span_rows, length, channels), 'col', s...]
    ppermute x0 -> x9, waiting for transfers between devices: none -> 12.5 us  [the longest x3 4.86 us: to_partner(): return lax.ppermute(array, 'row', [(r, r ^ 1) for r in range(row_count)])]
    ppermute x0 -> x9, starting transfers between devices: none -> 9.54 us  [the longest x4 6.21 us: moved(): return lax.ppermute(array, 'col', [(c, c ^ dc) for c in range(col_count)])]
    dot_general x22 -> x0, matrix products: 8.3 us -> none  [the longest x4 1.84 us: attend(): jnp.einsum('ehqd,ehkd->ehqk', queries, key_rows, preferred_element_type=j...]
    while x36 -> x0, local copies, waits for them, and re-layouts: 4.52 us -> none
  transfers between devices with their start and end apart: 8 -> 9, of which waited for: 8 -> 8; matrix products, arithmetic and copies ran while one was open for 5% -> 1% of each run, Pallas kernels for 0% -> 0%
where the time goes in v1:
time: 90.9 us; the launch traced here: 90.6 us
  Pallas kernels  63.5 us (70%)
  waiting for transfers between devices  12.5 us (14%)
  starting transfers between devices  9.54 us (10%)
  local copies, waits for them, and re-layouts  3.36 us (4%)
  other arithmetic  1.61 us (2%)
    pallas_call x4, Pallas kernels, call(): pl.pallas_call(kernel, grid=(1,), in_specs=[whole(array.shape) for array...  63.5 us
    ppermute x4, starting transfers between devices, moved(): return lax.ppermute(array, 'col', [(c, c ^ dc) for c in range(col_count)])  6.21 us
    ppermute x3, waiting for transfers between devices, to_partner(): return lax.ppermute(array, 'row', [(r, r ^ 1) for r in range(row_count)])  4.86 us
    ppermute x4, waiting for transfers between devices, moved(): return lax.ppermute(array, 'col', [(c, c ^ dc) for c in range(col_count)])  4.77 us
    unnamed x20, local copies, waits for them, and re-layouts  3.36 us
    ppermute x1, starting transfers between devices, moved(): return lax.ppermute(array, ('row', 'col'), routes)  2.51 us
  transfers between devices with their start and end apart: 9, of which 8 were waited for; matrix products, arithmetic and copies ran while one was open for 1% of the time, Pallas kernels for 0%

profile of v1, /device:TPU:0, one launch (start us, length us, event | category | flops | bytes accessed | tf_op | source)
XLA Modules:
  0.0 90.6 jit_solution(896681108370142132)
XLA Ops:
  0.0 5.1 %collective-permute-start.2 = (bf16[8,2,8,128]{3,2,1,0:T(8,128)(2,1)}, bf16[8,2,8,128]{3,2,1,0:T(8,128)(2,1)S(1)}, u32[]{:S(2)}, u32[]{:S(2)}) collective-permute-start(bf16[8,2,8,128]{3,2,1,0:T(8,128)(2,1)} %bitcast.7), channel_id=1, source_target_pairs={{0,6},{1,7},{2,4},{3,5},{4,2},{5,3},{6,0},{7,1},{8,14},{9,15},{10,... | collective-permute-start | bytes 98312 | tf_op jit(solution)/shard_map/ppermute | solution.py:456
  5.1 0.0 collective-permute-start.1
  5.1 0.6 collective-permute-start
  5.7 1.5 %collective-permute-done.2 = bf16[8,2,8,128]{3,2,1,0:T(8,128)(2,1)S(1)} collective-permute-done((bf16[8,2,8,128]{3,2,1,0:T(8,128)(2,1)}, bf16[8,2,8,128]{3,2,1,0:T(8,128)(2,1)S(1)}, u32[]{:S(2)}, u32[]{:S(2)}) %collective-permute-start.2) | collective-permute-done | bytes 32800 | tf_op jit(solution)/shard_map/ppermute | solution.py:456
  7.2 2.9 %collective-permute-done.1 = bf16[8,2,8,128]{3,2,1,0:T(8,128)(2,1)S(1)} collective-permute-done((bf16[8,2,8,128]{3,2,1,0:T(8,128)(2,1)}, bf16[8,2,8,128]{3,2,1,0:T(8,128)(2,1)S(1)}, u32[]{:S(2)}, u32[]{:S(2)}) %collective-permute-start.1) | collective-permute-done | bytes 32800 | tf_op jit(solution)/shard_map/ppermute | solution.py:456
  10.1 0.0 collective-permute-done
  10.1 0.8 pad_maximum_fusion.refs_0_
  10.9 0.0 copy-start
  10.9 2.5 %collective-permute-start.5 = (bf16[4,8,2,8,128]{4,3,2,1,0:T(8,128)(2,1)S(1)}, bf16[4,8,2,8,128]{4,3,2,1,0:T(8,128)(2,1)S(1)}, u32[]{:S(2)}, u32[]{:S(2)}) collective-permute-start(bf16[4,8,2,8,128]{4,3,2,1,0:T(8,128)(2,1)S(1)} %pad_maximum_fusion.refs_0_), channel_id=1, source_target_pairs={{0,17},{1,16},{2,19},{3,18},{4,21},{5,20},{6,23},{7,22},{8,25},{9,... | collective-permute-start | bytes 393224 | tf_op jit(solution)/shard_map/ppermute | solution.py:463
  13.4 0.5 collective-permute-start.4
  14.0 0.5 collective-permute-start.3
  14.5 0.2 copy.9
  14.7 0.2 copy.10
  14.8 0.8 maximum_bitcast_fusion.refs_6_.w_value_gate
  15.7 1.5 %collective-permute-done.5.refs_3_ = bf16[4,8,2,8,128]{4,3,2,1,0:T(8,128)(2,1)S(1)} collective-permute-done((bf16[4,8,2,8,128]{4,3,2,1,0:T(8,128)(2,1)S(1)}, bf16[4,8,2,8,128]{4,3,2,1,0:T(8,128)(2,1)S(1)}, u32[]{:S(2)}, u32[]{:S(2)}) %collective-permute-start.5) | collective-permute-done | bytes 131104 | tf_op jit(solution)/shard_map/ppermute | solution.py:463
  17.2 1.4 %collective-permute-done.4.refs_2_ = bf16[4,8,2,8,128]{4,3,2,1,0:T(8,128)(2,1)S(1)} collective-permute-done((bf16[4,8,2,8,128]{4,3,2,1,0:T(8,128)(2,1)S(1)}, bf16[4,8,2,8,128]{4,3,2,1,0:T(8,128)(2,1)S(1)}, u32[]{:S(2)}, u32[]{:S(2)}) %collective-permute-start.4) | collective-permute-done | bytes 131104 | tf_op jit(solution)/shard_map/ppermute | solution.py:458
  18.6 0.4 collective-permute-done.3.refs_1_
  18.9 0.3 copy-done.7
  19.2 0.6 copy-done.8
  19.8 18.7 %shard_map.82 = (bf16[32,32,128]{2,1,0:T(8,128)(2,1)}, bf16[32,32,128]{2,1,0:T(8,128)(2,1)}) custom-call(bf16[4,8,2,8,128]{4,3,2,1,0:T(8,128)(2,1)} %copy-done.2, bf16[4,8,2,8,128]{4,3,2,1,0:T(8,128)(2,1)} %copy-done.8, bf16[4,8,2,8,128]{4,3,2,1,0:T(8,128)(2,1)} %copy-done.7, bf16[4,8,2,8,128]{4,3,2,1,0:T(8,128)(2,1)} %copy-done.6, ...), custom_call_target="tpu_custom_call" | custom-call | tf_op jit(solution)/shard_map/pallas_call | solution.py:431
  38.6 0.0 collective-permute-start.6
  38.6 1.7 %collective-permute-done.6.recv = bf16[32,32,128]{2,1,0:T(8,128)(2,1)S(1)} collective-permute-done((bf16[32,32,128]{2,1,0:T(8,128)(2,1)}, bf16[32,32,128]{2,1,0:T(8,128)(2,1)S(1)}, u32[]{:S(2)}, u32[]{:S(2)}) %collective-permute-start.6) | collective-permute-done | bytes 262176 | tf_op jit(solution)/shard_map/ppermute | solution.py:466
  40.3 0.7 copy-done.3
  41.0 18.4 %shard_map.83 = (bf16[32,64,128]{2,1,0:T(8,128)(2,1)}, bf16[32,32,128]{2,1,0:T(8,128)(2,1)}, bf16[32,32,128]{2,1,0:T(8,128)(2,1)}) custom-call(bf16[32,32,128]{2,1,0:T(8,128)(2,1)} %get-tuple-element.12.keep, bf16[32,32,128]{2,1,0:T(8,128)(2,1)} %copy-done.3, bf16[2,2,128,256]{3,2,1,0:T(8,128)(2,1)} %w_query.5, bf16[2,2,128,256]{3,2,1,0:T(8,128)(2,1)} %w_key.5, ...), custom_call_target="tpu_custom_call" | custom-call | tf_op jit(solution)/shard_map/pallas_call | solution.py:431
  59.4 0.1 collective-permute-start.7
  59.5 1.6 %collective-permute-done.7.recv = bf16[32,32,128]{2,1,0:T(8,128)(2,1)S(1)} collective-permute-done((bf16[32,32,128]{2,1,0:T(8,128)(2,1)}, bf16[32,32,128]{2,1,0:T(8,128)(2,1)S(1)}, u32[]{:S(2)}, u32[]{:S(2)}) %collective-permute-start.7) | collective-permute-done | bytes 262176 | tf_op jit(solution)/shard_map/ppermute | solution.py:466
  61.1 0.7 copy-done.4
  61.8 21.8 %shard_map.84 = (bf16[24,32,128]{2,1,0:T(8,128)(2,1)}, bf16[24,32,128]{2,1,0:T(8,128)(2,1)}) custom-call(bf16[32,64,128]{2,1,0:T(8,128)(2,1)} %get-tuple-element.14.slab, bf16[32,32,128]{2,1,0:T(8,128)(2,1)} %get-tuple-element.15.own, bf16[32,32,128]{2,1,0:T(8,128)(2,1)} %copy-done.4, bf16[2,128,512]{2,1,0:T(8,128)(2,1)} %w_in.3, ...), custom_call_target="tpu_custom_call" | custom-call | tf_op jit(solution)/shard_map/pallas_call | solution.py:431
  83.7 0.1 collective-permute-start.8
  83.8 1.5 %collective-permute-done.8.recv = bf16[24,32,128]{2,1,0:T(8,128)(2,1)S(1)} collective-permute-done((bf16[24,32,128]{2,1,0:T(8,128)(2,1)}, bf16[24,32,128]{2,1,0:T(8,128)(2,1)S(1)}, u32[]{:S(2)}, u32[]{:S(2)}) %collective-permute-start.8) | collective-permute-done | bytes 196640 | tf_op jit(solution)/shard_map/ppermute | solution.py:466
  85.3 0.7 copy-done.5
  86.0 4.6 %shard_map.85 = bf16[8,1,2,8,128]{4,3,2,1,0:T(8,128)(2,1)} custom-call(bf16[24,32,128]{2,1,0:T(8,128)(2,1)} %get-tuple-element.17.keep, bf16[24,32,128]{2,1,0:T(8,128)(2,1)} %copy-done.5, bf16[2,2,128,256]{3,2,1,0:T(8,128)(2,1)} %w_query.5, bf16[2,2,128,256]{3,2,1,0:T(8,128)(2,1)} %w_key.5, bf16[2,2,128,256]{3,2,1,0:T(8,128)(2,1)} %w_value.1, ...), custom_call_target="tpu_custom_call" | custom-call | tf_op jit(solution)/shard_map/pallas_call | solution.py:431
  (12 shorter events, 0.0 us)
Async XLA Ops:
  0.0 14.5 %copy-start.1 = (bf16[2,2,128,256]{3,2,1,0:T(8,128)(2,1)S(1)}, bf16[2,2,128,256]{3,2,1,0:T(8,128)(2,1)}, u32[]{:S(2)}) copy-start(bf16[2,2,128,256]{3,2,1,0:T(8,128)(2,1)} %w_value.1) | copy-start | bytes 786436
  0.0 7.2 %collective-permute-start.2 = (bf16[8,2,8,128]{3,2,1,0:T(8,128)(2,1)}, bf16[8,2,8,128]{3,2,1,0:T(8,128)(2,1)S(1)}, u32[]{:S(2)}, u32[]{:S(2)}) collective-permute-start(bf16[8,2,8,128]{3,2,1,0:T(8,128)(2,1)} %bitcast.7), channel_id=1, source_target_pairs={{0,6},{1,7},{2,4},{3,5},{4,2},{5,3},{6,0},{7,1},{8,14},{9,15},{10,... | collective-permute-start | bytes 98312 | tf_op jit(solution)/shard_map/ppermute | solution.py:456
  5.1 5.0 %collective-permute-start.1 = (bf16[8,2,8,128]{3,2,1,0:T(8,128)(2,1)}, bf16[8,2,8,128]{3,2,1,0:T(8,128)(2,1)S(1)}, u32[]{:S(2)}, u32[]{:S(2)}) collective-permute-start(bf16[8,2,8,128]{3,2,1,0:T(8,128)(2,1)} %bitcast.8), channel_id=1, source_target_pairs={{0,4},{1,5},{2,6},{3,7},{4,0},{5,1},{6,2},{7,3},{8,12},{9,13},{10,... | collective-permute-start | bytes 98312 | tf_op jit(solution)/shard_map/ppermute | solution.py:456
  5.1 5.0 %collective-permute-start = (bf16[8,2,8,128]{3,2,1,0:T(8,128)(2,1)}, bf16[8,2,8,128]{3,2,1,0:T(8,128)(2,1)S(1)}, u32[]{:S(2)}, u32[]{:S(2)}) collective-permute-start(bf16[8,2,8,128]{3,2,1,0:T(8,128)(2,1)} %bitcast.9), channel_id=1, source_target_pairs={{0,2},{1,3},{2,0},{3,1},{4,6},{5,7},{6,4},{7,5},{8,10},{9,11},{10,... | collective-permute-start | bytes 98312 | tf_op jit(solution)/shard_map/ppermute | solution.py:456
  10.9 3.8 %copy-start.2 = (bf16[4,8,2,8,128]{4,3,2,1,0:T(8,128)(2,1)}, bf16[4,8,2,8,128]{4,3,2,1,0:T(8,128)(2,1)S(1)}, u32[]{:S(2)}) copy-start(bf16[4,8,2,8,128]{4,3,2,1,0:T(8,128)(2,1)S(1)} %pad_maximum_fusion.refs_0_) | copy-start | bytes 393220
  10.9 3.8 %copy-start = (bf16[2,2,128,256]{3,2,1,0:T(8,128)(2,1)S(1)}, bf16[2,2,128,256]{3,2,1,0:T(8,128)(2,1)}, u32[]{:S(2)}) copy-start(bf16[2,2,128,256]{3,2,1,0:T(8,128)(2,1)} %w_gate.1) | copy-start | bytes 786436
  10.9 6.3 %collective-permute-start.5 = (bf16[4,8,2,8,128]{4,3,2,1,0:T(8,128)(2,1)S(1)}, bf16[4,8,2,8,128]{4,3,2,1,0:T(8,128)(2,1)S(1)}, u32[]{:S(2)}, u32[]{:S(2)}) collective-permute-start(bf16[4,8,2,8,128]{4,3,2,1,0:T(8,128)(2,1)S(1)} %pad_maximum_fusion.refs_0_), channel_id=1, source_target_pairs={{0,17},{1,16},{2,19},{3,18},{4,21},{5,20},{6,23},{7,22},{8,25},{9,... | collective-permute-start | bytes 393224 | tf_op jit(solution)/shard_map/ppermute | solution.py:463
  13.4 5.1 %collective-permute-start.4 = (bf16[4,8,2,8,128]{4,3,2,1,0:T(8,128)(2,1)S(1)}, bf16[4,8,2,8,128]{4,3,2,1,0:T(8,128)(2,1)S(1)}, u32[]{:S(2)}, u32[]{:S(2)}) collective-permute-start(bf16[4,8,2,8,128]{4,3,2,1,0:T(8,128)(2,1)S(1)} %pad_maximum_fusion.refs_0_), channel_id=1, source_target_pairs={{0,16},{8,24},{16,0},{24,8},{1,17},{9,25},{17,1},{25,9},{2,18},{10... | collective-permute-start | bytes 393224 | tf_op jit(solution)/shard_map/ppermute | solution.py:458
  14.0 5.0 %collective-permute-start.3 = (bf16[4,8,2,8,128]{4,3,2,1,0:T(8,128)(2,1)S(1)}, bf16[4,8,2,8,128]{4,3,2,1,0:T(8,128)(2,1)S(1)}, u32[]{:S(2)}, u32[]{:S(2)}) collective-permute-start(bf16[4,8,2,8,128]{4,3,2,1,0:T(8,128)(2,1)S(1)} %pad_maximum_fusion.refs_0_), channel_id=1, source_target_pairs={{0,1},{1,0},{2,3},{3,2},{4,5},{5,4},{6,7},{7,6},{8,9},{9,8},{10,11... | collective-permute-start | bytes 393224 | tf_op jit(solution)/shard_map/ppermute | solution.py:456
  17.2 1.7 %copy-start.6 = (bf16[4,8,2,8,128]{4,3,2,1,0:T(8,128)(2,1)}, bf16[4,8,2,8,128]{4,3,2,1,0:T(8,128)(2,1)S(1)}, u32[]{:S(2)}) copy-start(bf16[4,8,2,8,128]{4,3,2,1,0:T(8,128)(2,1)S(1)} %collective-permute-done.5.refs_3_) | copy-start | bytes 393220
  18.5 0.7 copy-start.7
  19.2 0.6 copy-start.8
  38.6 1.7 %collective-permute-start.6 = (bf16[32,32,128]{2,1,0:T(8,128)(2,1)}, bf16[32,32,128]{2,1,0:T(8,128)(2,1)S(1)}, u32[]{:S(2)}, u32[]{:S(2)}) collective-permute-start(bf16[32,32,128]{2,1,0:T(8,128)(2,1)} %get-tuple-element.13), channel_id=1, source_target_pairs={{0,8},{8,0},{16,24},{24,16},{1,9},{9,1},{17,25},{25,17},{2,10},{10... | collective-permute-start | bytes 786440 | tf_op jit(solution)/shard_map/ppermute | solution.py:466
  40.3 0.7 copy-start.3
  59.4 1.7 %collective-permute-start.7 = (bf16[32,32,128]{2,1,0:T(8,128)(2,1)}, bf16[32,32,128]{2,1,0:T(8,128)(2,1)S(1)}, u32[]{:S(2)}, u32[]{:S(2)}) collective-permute-start(bf16[32,32,128]{2,1,0:T(8,128)(2,1)} %get-tuple-element.16), channel_id=1, source_target_pairs={{0,8},{8,0},{16,24},{24,16},{1,9},{9,1},{17,25},{25,17},{2,10},{10... | collective-permute-start | bytes 786440 | tf_op jit(solution)/shard_map/ppermute | solution.py:466
  61.1 0.7 copy-start.4
  83.7 1.7 %collective-permute-start.8 = (bf16[24,32,128]{2,1,0:T(8,128)(2,1)}, bf16[24,32,128]{2,1,0:T(8,128)(2,1)S(1)}, u32[]{:S(2)}, u32[]{:S(2)}) collective-permute-start(bf16[24,32,128]{2,1,0:T(8,128)(2,1)} %get-tuple-element.18), channel_id=1, source_target_pairs={{0,8},{8,0},{16,24},{24,16},{1,9},{9,1},{17,25},{25,17},{2,10},{10... | collective-permute-start | bytes 589832 | tf_op jit(solution)/shard_map/ppermute | solution.py:466
  85.3 0.7 copy-start.5

commit v2 on v1

--- a/solution.py
+++ b/solution.py
@@ -11,6 +11,7 @@
 HEADS = 8
 HEAD_DIM = 32
 LANES = 128
+SUBLANES = 8
 VMEM_BUDGET = 24 * 2**20
 
 
@@ -144,79 +145,88 @@
 
 
 def project(normed, span, weights, stores):
-    w_query, w_key, w_value_gate = weights
-    queries, keys, values, gates = stores
-    inner = w_query.shape[1]
-    queries[span, :] = dot(normed, w_query[...]).astype(jnp.bfloat16)
+    w_key, w_rest = weights
+    queries, keys, values, gates = stores[:4]
+    inner = w_key.shape[1]
     keys[span, :] = dot(normed, w_key[...]).astype(jnp.bfloat16)
-    values[:, span] = dot(w_value_gate[:inner, :], normed, NT).astype(jnp.bfloat16)
-    gates[:, span] = jax.nn.sigmoid(dot(w_value_gate[inner:, :], normed, NT))
-
-
-def attend_pair(start, length, stores, w_out):
-    queries, keys, values, gates = stores
+    queries[:, span] = dot(w_rest[:inner, :], normed, NT).astype(jnp.bfloat16)
+    values[:, span] = dot(w_rest[inner : 2 * inner, :], normed, NT).astype(jnp.bfloat16)
+    gates[:, span] = 0.5 * jnp.tanh(0.5 * dot(w_rest[2 * inner :, :], normed, NT)) + 0.5
+
+
+def lane_halves(length):
+    lane = lax.broadcasted_iota(jnp.int32, (1, 2 * LANES), 1) % LANES
+    low = (lane < length).astype(jnp.float32).astype(jnp.bfloat16)
+    high = (lane >= length).astype(jnp.float32).astype(jnp.bfloat16)
+    return low, high
+
+
+def softmax_tile(tile, start, length, stores, probs, inverses):
+    queries, keys = stores[:2]
+    low, high = lane_halves(length)
+    scale = HEAD_DIM ** (-0.5) * math.log2(math.e)
+    per_group = LANES // HEAD_DIM
     both = pl.ds(start, 2 * length)
-    per_group = LANES // HEAD_DIM
-    groups = HEADS // per_group
-    scale = HEAD_DIM ** (-0.5) * math.log2(math.e)
-    lane = lax.broadcasted_iota(jnp.int32, (1, LANES), 1)
-    head_masks = [
-        (lane // HEAD_DIM == h).astype(jnp.float32).astype(jnp.bfloat16) for h in range(per_group)
-    ]
-    low = lane < length
-    low_mask = low.astype(jnp.float32).astype(jnp.bfloat16)
-    high_mask = (~low).astype(jnp.float32).astype(jnp.bfloat16)
-    gated = [None] * HEADS
-    for group in range(groups):
-        channels = slice(group * LANES, (group + 1) * LANES)
-        probs, denominators = [], []
-        for which in range(2):
-            rows = pl.ds(start + which * length, length)
-            query = queries[rows, channels]
-            order = [h ^ which for h in range(per_group)]
-            spread = jnp.concatenate([query * head_masks[h] for h in order], axis=0)
-            scores = dot(keys[rows, channels], spread, NT)
-            exponent = jnp.exp2((scores - jnp.max(scores, axis=0, keepdims=True)) * scale)
-            denominators.append(jnp.sum(exponent, axis=0, keepdims=True))
-            probs.append(exponent.astype(jnp.bfloat16))
-        for tile in range(per_group // 2):
-            columns = slice(tile * LANES, (tile + 1) * LANES)
-            first, second = probs[0][:, columns], probs[1][:, columns]
-            spread = jnp.concatenate(
-                [
-                    jnp.concatenate([first * low_mask, second * high_mask], axis=0),
-                    jnp.concatenate([first * high_mask, second * low_mask], axis=0),
-                ],
-                axis=1,
-            )
-            head = group * per_group + 2 * tile
-            inner = slice(head * HEAD_DIM, (head + 2) * HEAD_DIM)
-            blended = dot(values[inner, both], spread)
-            one, two = denominators[0][:, columns], denominators[1][:, columns]
-            even = blended[:HEAD_DIM, :LANES] / jnp.where(low, one, two)
-            odd = blended[HEAD_DIM:, LANES:] / jnp.where(low, two, one)
-            odd = pltpu.roll(odd, length, 1)
-            gate = gates[inner, both]
-            gated[head] = (gate[:HEAD_DIM] * even).astype(jnp.bfloat16)
-            gated[head + 1] = (gate[HEAD_DIM:] * odd).astype(jnp.bfloat16)
-    return dot(jnp.concatenate(gated, axis=0), w_out[...], TN)
+    first_rows = pl.ds(start, length)
+    second_rows = pl.ds(start + length, length)
+    group = 2 * tile // per_group
+    channels = slice(group * LANES, (group + 1) * LANES)
+    key = jnp.concatenate([keys[first_rows, channels], keys[second_rows, channels]], axis=1)
+    blank = jnp.zeros((HEAD_DIM, LANES), jnp.bfloat16)
+    columns = []
+    for head in (2 * tile, 2 * tile + 1):
+        query = queries[head * HEAD_DIM : (head + 1) * HEAD_DIM, both]
+        column = [blank] * (2 * per_group)
+        column[head % per_group] = query * low[:, :LANES]
+        column[per_group + head % per_group] = query * high[:, :LANES]
+        columns.append(jnp.concatenate(column, axis=0))
+    scores = dot(key, jnp.concatenate(columns, axis=1))
+    exponent = jnp.exp2((scores - jnp.max(scores, axis=0, keepdims=True)) * scale)
+    inverses[tile] = 1.0 / jnp.sum(exponent, axis=0, keepdims=True)
+    probs[tile] = exponent.astype(jnp.bfloat16)
+
+
+def blend_tile(tile, start, length, stores, probs, inverses):
+    values, gates, gated = stores[2:5]
+    low, high = lane_halves(length)
+    both = pl.ds(start, 2 * length)
+    inner = slice(2 * tile * HEAD_DIM, 2 * (tile + 1) * HEAD_DIM)
+    prob, inverse = probs[tile], inverses[tile]
+    blended = dot(values[inner, both], jnp.concatenate([prob * low, prob * high], axis=0))
+    blended = jnp.concatenate(
+        [
+            blended[:HEAD_DIM, :LANES] * inverse[:, :LANES],
+            blended[HEAD_DIM:, LANES:] * inverse[:, LANES:],
+        ],
+        axis=0,
+    )
+    gated[inner, both] = (gates[inner, both] * blended).astype(jnp.bfloat16)
 
 
 def rounded(values):
     return values.astype(jnp.bfloat16).astype(jnp.float32)
 
 
-def attend_slab(grid, length, stores, w_out, unroll):
-    pair = 2 * length
-
-    def step(index, carry):
-        start = pl.multiple_of(index * pair, pair)
-        update = attend_pair(start, length, stores, w_out)
-        here = pl.ds(start, pair)
-        grid[here, :] = rounded(grid[here, :] + update)
-        return carry
-
-    lax.fori_loop(0, grid.shape[0] // pair, step, 0, unroll=unroll)
+def attend_slab(length, weights, stores):
+    w_key, w_rest, w_out = weights
+    gated, grid, turned, probs, inverses = stores[4:]
+    half = grid.shape[0] // length
+    project(layer_norm(grid[...]), pl.ds(0, grid.shape[0]), (w_key, w_rest), stores)
+    for phase in (softmax_tile, blend_tile):
+        for pair in range(half // 2):
+            for tile in range(HEADS // 2):
+                phase(tile, pair * 2 * length, length, stores, probs.at[pair], inverses.at[pair])
+    result = grid[...] + dot(gated[...], w_out[...], TN)
+    for seq in range(half):
+        for at in range(length // SUBLANES):
+            start = (at * half + seq) * SUBLANES
+            row = seq * length + at * SUBLANES
+            turned[start : start + SUBLANES, :] = result[row : row + SUBLANES]
+
+
+def position(turned, half, at):
+    start = (at // SUBLANES) * (half * SUBLANES) + at % SUBLANES
+    return turned[pl.ds(start, half, stride=SUBLANES), :].astype(jnp.bfloat16)
 
 
 def transition(values, w_in, w_back):
@@ -227,8 +237,9 @@
 def first_row_kernel(dims, *refs):
     blocks, pairs, span, width = dims
     parts = refs[:4]
-    w_query, w_key, w_value_gate, w_out, keep, send, grid = refs[4:11]
-    stores = refs[11:15]
+    w_key, w_rest, w_out, keep, send = refs[4:9]
+    stores = refs[9:]
+    grid, turned = stores[5:7]
     row, col = lax.axis_index("row"), lax.axis_index("col")
     x, core = row // 2, row % 2
     length = blocks * width
@@ -244,88 +255,60 @@
                     grid[pl.ds(pl.multiple_of(at, width), width), :] = part[other, a, e].astype(
                         jnp.float32
                     )
-    chunk = 4 * length
-
-    def step(index, carry):
-        here = pl.ds(pl.multiple_of(index * chunk, chunk), chunk)
-        project(layer_norm(grid[here, :]), here, (w_query, w_key, w_value_gate), stores)
-        return carry
-
-    lax.fori_loop(0, grid.shape[0] // chunk, step, 0)
-    attend_slab(grid, length, stores, w_out, 2)
+    attend_slab(length, (w_key, w_rest, w_out), stores)
     for target, parity in ((keep, core), (send, 1 - core)):
         for a in range(blocks):
             for other in range(pairs):
                 for e in range(span):
                     at = a * width + other * 2 * span + parity * span + e
-                    target[(a * pairs + other) * span + e] = grid[
-                        pl.ds(at, half, stride=length), :
-                    ].astype(jnp.bfloat16)
-
-
-def col_kernel(keep, recv, w_query, w_key, w_value_gate, w_out, slab, own, send, grid, *stores):
+                    target[(a * pairs + other) * span + e] = position(turned, half, at)
+
+
+def col_kernel(keep, recv, w_key, w_rest, w_out, slab, own, send, *stores):
+    grid, turned = stores[5:7]
     half = keep.shape[1]
     length = 2 * half
-    count = 4
-
-    def step(index, carry):
-        seqs = pl.ds(index * count, count)
-        values = jnp.concatenate([keep[seqs], recv[seqs]], axis=1).astype(jnp.float32)
-        values = values.reshape(count * length, values.shape[2])
-        here = pl.ds(pl.multiple_of(index * count * length, count * length), count * length)
-        grid[here, :] = values
-        project(layer_norm(values), here, (w_query, w_key, w_value_gate), stores)
-        return carry
-
-    lax.fori_loop(0, half // count, step, 0)
-    attend_slab(grid, length, stores, w_out, 2)
+    both = jnp.concatenate([keep[...], recv[...]], axis=1).astype(jnp.float32)
+    grid[...] = both.reshape(grid.shape)
+    attend_slab(length, (w_key, w_rest, w_out), stores)
+    groups = length // SUBLANES
     for j in range(half):
-        slab[j] = grid[j * length : (j + 1) * length, :].astype(jnp.bfloat16)
+        for at in range(0, groups, 2):
+            rows = [(at + k) * half * SUBLANES + j * SUBLANES for k in range(2)]
+            slab[j, at * SUBLANES : (at + 2) * SUBLANES] = jnp.concatenate(
+                [turned[row : row + SUBLANES, :] for row in rows], axis=0
+            ).astype(jnp.bfloat16)
     for i in range(half):
-        own[i] = grid[pl.ds(i, half, stride=length), :].astype(jnp.bfloat16)
-        send[i] = grid[pl.ds(half + i, half, stride=length), :].astype(jnp.bfloat16)
+        own[i] = position(turned, half, i)
+        send[i] = position(turned, half, half + i)
 
 
 def mid_row_kernel(
-    dims, slab, own, recv, w_in, w_back, w_query, w_key, w_value_gate, w_out, keep, send, grid, *stores
+    dims, slab, own, recv, w_in, w_back, w_key, w_rest, w_out, keep, send, *stores
 ):
+    grid, turned = stores[5:7]
     blocks, pairs, span, width = dims
     half = own.shape[0]
     length = 2 * half
-    count = 4
     row, col = lax.axis_index("row"), lax.axis_index("col")
     x, core = row // 2, row % 2
-
-    def step(index, carry):
-        seqs = pl.ds(index * count, count)
-        direct = jnp.concatenate([own[seqs], recv[seqs]], axis=1).astype(jnp.float32)
-        values = rounded(0.5 * (direct + slab[seqs].astype(jnp.float32)))
-        values = transition(values.reshape(count * length, values.shape[2]), w_in, w_back)
-        here = pl.ds(pl.multiple_of(index * count * length, count * length), count * length)
-        grid[here, :] = values
-        project(layer_norm(values), here, (w_query, w_key, w_value_gate), stores)
-        return carry
-
-    lax.fori_loop(0, half // count, step, 0)
-    attend_slab(grid, length, stores, w_out, 2)
+    direct = jnp.concatenate([own[...], recv[...]], axis=1).astype(jnp.float32)
+    values = rounded(0.5 * (direct + slab[...].astype(jnp.float32)))
+    grid[...] = transition(values.reshape(grid.shape), w_in, w_back)
+    attend_slab(length, (w_key, w_rest, w_out), stores)
     for other in range(pairs):
         for k in range(2):
             for e in range(span):
                 number = (other * 2 + k) * span + e
-                inside = (col * pairs + other) * span + e
-                for target, mine in ((keep, core), (send, 1 - core)):
-                    at = inside + half * (k ^ mine)
-                    if target is send:
-                        at = inside + half * (k ^ core)
-                    else:
-                        at = inside + half * (k ^ core)
-                    target[number] = grid[pl.ds(at, half, stride=length), :].astype(jnp.bfloat16)
+                column = position(turned, half, half * (k ^ core) + (col * pairs + other) * span + e)
+                keep[number] = column
+                send[number] = column
     for a in range(blocks):
         for e in range(span):
             inside = (a * pairs + x) * span + e
             number = width + a * span + e
-            keep[number] = grid[pl.ds(inside, half, stride=length), :].astype(jnp.bfloat16)
-            send[number] = grid[pl.ds(half + inside, half, stride=length), :].astype(jnp.bfloat16)
+            keep[number] = position(turned, half, inside)
+            send[number] = position(turned, half, half + inside)
 
 
 def few_queries(query, keys, values, head_masks, tile_masks):
@@ -449,7 +432,7 @@
     positions = half * length
     dims = (blocks, pairs, span, width)
     tile = pair.reshape(blocks, span, width, channels)
-    w_value_gate = jnp.swapaxes(jnp.concatenate([w_value, w_gate], axis=3), 2, 3)
+    w_rest = jnp.swapaxes(jnp.concatenate([w_query, w_value, w_gate], axis=3), 2, 3)
 
     def moved(array, dx, dc):
         if dx == 0:
@@ -472,19 +455,22 @@
             parts.append(near if dx == dy == 0 else moved(near, dx, dy))
 
     f32, bf16 = jnp.float32, jnp.bfloat16
-    grid = pltpu.VMEM((positions, channels), f32)
     stores = [
-        pltpu.VMEM((positions, inner), bf16),
+        pltpu.VMEM((inner, positions), bf16),
         pltpu.VMEM((positions, inner), bf16),
         pltpu.VMEM((inner, positions), bf16),
         pltpu.VMEM((inner, positions), f32),
+        pltpu.VMEM((inner, positions), bf16),
+        pltpu.VMEM((positions, channels), f32),
+        pltpu.VMEM((positions, channels), f32),
+        pltpu.VMEM((half // 2, HEADS // 2, length, 2 * LANES), bf16),
+        pltpu.VMEM((half // 2, HEADS // 2, 1, 2 * LANES), f32),
     ]
 
     def attention(layer, direction):
         return [
-            (w_query, layer, direction),
             (w_key, layer, direction),
-            (w_value_gate, layer, direction),
+            (w_rest, layer, direction),
             (w_out, layer, direction),
         ]
 
@@ -494,7 +480,7 @@
         parts,
         attention(0, 0),
         [quadrant, quadrant],
-        [grid] + stores,
+        stores,
     )
     layers = w_in.shape[0]
     for layer in range(layers - 1):
@@ -503,7 +489,7 @@
             [keep, to_partner(send)],
             attention(layer, 1),
             [(half, length, channels), quadrant, quadrant],
-            [grid] + stores,
+            stores,
         )
         last = layer == layers - 2
         few = (width + blocks * span, half, channels)
@@ -512,7 +498,7 @@
             [slab, own, to_partner(send)],
             [(w_in, layer), (w_back, layer)] + attention(layer + 1, 0),
             [few, few],
-            [grid] + stores,
+            stores,
         )
     layer = layers - 1
     seqs = width + blocks * span

time: 90.9 us -> 52.9 us (0.58)
  Pallas kernels: 63.5 us -> 26.3 us
  waiting for transfers between devices: 12.5 us -> 10.3 us
  local copies, waits for them, and re-layouts: 3.36 us -> 5.43 us
    pallas_call x4, Pallas kernels: 63.5 us -> 26.3 us  [call(): pl.pallas_call(kernel, grid=(1,), in_specs=[whole(array.shape) for array...]
    ppermute x4, waiting for transfers between devices: 4.77 us -> 2.32 us  [moved(): return lax.ppermute(array, 'col', [(c, c ^ dc) for c in range(col_count)])]
    unnamed x20 -> x21, local copies, waits for them, and re-layouts: 3.36 us -> 5.43 us
  transfers between devices with their start and end apart: 9 -> 9, of which waited for: 8 -> 7; matrix products, arithmetic and copies ran while one was open for 1% -> 6% of each run, Pallas kernels for 0% -> 0%
where the time goes in v2:
time: 52.9 us; the launch traced here: 52.6 us
  Pallas kernels  26.3 us (50%)
  waiting for transfers between devices  10.3 us (19%)
  starting transfers between devices  9.54 us (18%)
  local copies, waits for them, and re-layouts  5.43 us (10%)
  other arithmetic  0.95 us (2%)
    pallas_call x4, Pallas kernels, call(): pl.pallas_call(kernel, grid=(1,), in_specs=[whole(array.shape) for array...  26.3 us
    ppermute x4, starting transfers between devices, moved(): return lax.ppermute(array, 'col', [(c, c ^ dc) for c in range(col_count)])  6.22 us
    unnamed x21, local copies, waits for them, and re-layouts  5.43 us
    ppermute x3, waiting for transfers between devices, to_partner(): return lax.ppermute(array, 'row', [(r, r ^ 1) for r in range(row_count)])  4.87 us
    ppermute x1, starting transfers between devices, moved(): return lax.ppermute(array, ('row', 'col'), routes)  2.51 us
    ppermute x4, waiting for transfers between devices, moved(): return lax.ppermute(array, 'col', [(c, c ^ dc) for c in range(col_count)])  2.32 us
    ppermute x1, waiting for transfers between devices, moved(): return lax.ppermute(array, ('row', 'col'), routes)  1.79 us
    ppermute x1, waiting for transfers between devices, moved(): lax.ppermute(array, 'row', [(r, r ^ 2 * dx) for r in range(row_count)])  1.36 us
  transfers between devices with their start and end apart: 9, of which 7 were waited for; matrix products, arithmetic and copies ran while one was open for 6% of the time, Pallas kernels for 0%

profile of v2, /device:TPU:0, one launch (start us, length us, event | category | flops | bytes accessed | tf_op | source)
XLA Modules:
  0.0 52.6 jit_solution(14087876057093019776)
XLA Ops:
  0.0 5.1 %collective-permute-start.2 = (bf16[8,2,8,128]{3,2,1,0:T(8,128)(2,1)}, bf16[8,2,8,128]{3,2,1,0:T(8,128)(2,1)S(1)}, u32[]{:S(2)}, u32[]{:S(2)}) collective-permute-start(bf16[8,2,8,128]{3,2,1,0:T(8,128)(2,1)} %bitcast.7), channel_id=1, source_target_pairs={{0,6},{1,7},{2,4},{3,5},{4,2},{5,3},{6,0},{7,1},{8,14},{9,15},{10,... | collective-permute-start | bytes 98312 | tf_op jit(solution)/shard_map/ppermute | solution.py:439
  5.1 0.0 collective-permute-start.1
  5.1 0.6 %collective-permute-start = (bf16[8,2,8,128]{3,2,1,0:T(8,128)(2,1)}, bf16[8,2,8,128]{3,2,1,0:T(8,128)(2,1)S(1)}, u32[]{:S(2)}, u32[]{:S(2)}) collective-permute-start(bf16[8,2,8,128]{3,2,1,0:T(8,128)(2,1)} %bitcast.9), channel_id=1, source_target_pairs={{0,2},{1,3},{2,0},{3,1},{4,6},{5,7},{6,4},{7,5},{8,10},{9,11},{10,... | collective-permute-start | bytes 98312 | tf_op jit(solution)/shard_map/ppermute | solution.py:439
  5.7 1.1 %copy.9 = bf16[2,2,128,256]{2,3,1,0:T(8,128)(2,1)S(1)} copy(bf16[2,2,128,256]{3,2,1,0:T(8,128)(2,1)} %w_query.1) | data formatting | bytes 524288 | tf_op args[1]
  6.8 1.1 %copy.10 = bf16[2,2,128,256]{2,3,1,0:T(8,128)(2,1)S(1)} copy(bf16[2,2,128,256]{3,2,1,0:T(8,128)(2,1)} %w_value.1) | data formatting | bytes 524288 | tf_op args[3]
  8.0 0.2 copy.11
  8.2 0.0 collective-permute-done.2
  8.2 1.9 %collective-permute-done.1 = bf16[8,2,8,128]{3,2,1,0:T(8,128)(2,1)S(1)} collective-permute-done((bf16[8,2,8,128]{3,2,1,0:T(8,128)(2,1)}, bf16[8,2,8,128]{3,2,1,0:T(8,128)(2,1)S(1)}, u32[]{:S(2)}, u32[]{:S(2)}) %collective-permute-start.1) | collective-permute-done | bytes 32800 | tf_op jit(solution)/shard_map/ppermute | solution.py:439
  10.1 0.0 collective-permute-done
  10.1 2.5 %collective-permute-start.5 = (bf16[4,8,2,8,128]{4,3,2,1,0:T(8,128)(2,1)S(1)}, bf16[4,8,2,8,128]{4,3,2,1,0:T(8,128)(2,1)S(1)}, u32[]{:S(2)}, u32[]{:S(2)}) collective-permute-start(bf16[4,8,2,8,128]{4,3,2,1,0:T(8,128)(2,1)S(1)} %pad_maximum_fusion.refs_0_), channel_id=1, source_target_pairs={{0,17},{1,16},{2,19},{3,18},{4,21},{5,20},{6,23},{7,22},{8,25},{9,... | collective-permute-start | bytes 393224 | tf_op jit(solution)/shard_map/ppermute | solution.py:446
  12.7 0.5 %collective-permute-start.4 = (bf16[4,8,2,8,128]{4,3,2,1,0:T(8,128)(2,1)S(1)}, bf16[4,8,2,8,128]{4,3,2,1,0:T(8,128)(2,1)S(1)}, u32[]{:S(2)}, u32[]{:S(2)}) collective-permute-start(bf16[4,8,2,8,128]{4,3,2,1,0:T(8,128)(2,1)S(1)} %pad_maximum_fusion.refs_0_), channel_id=1, source_target_pairs={{0,16},{8,24},{16,0},{24,8},{1,17},{9,25},{17,1},{25,9},{2,18},{10... | collective-permute-start | bytes 393224 | tf_op jit(solution)/shard_map/ppermute | solution.py:441
  13.2 0.5 collective-permute-start.3
  13.7 0.9 %maximum_bitcast_fusion.refs_5_.w_rest = bf16[2,2,768,128]{3,2,1,0:T(8,128)(2,1)} fusion(bf16[2,2,128,256]{2,3,1,0:T(8,128)(2,1)S(1)} %copy.11, bf16[2,2,128,256]{2,3,1,0:T(8,128)(2,1)S(1)} %copy.10, bf16[2,2,128,256]{2,3,1,0:T(8,128)(2,1)S(1)} %copy.9), kind=kLoop, calls=%fused_computation | loop fusion | flops 2359296 | bytes 1572864 | tf_op jit(solution)/shard_map/transpose | solution.py:435
  14.6 0.0 copy-done.1
  14.6 1.8 %collective-permute-done.5.refs_3_ = bf16[4,8,2,8,128]{4,3,2,1,0:T(8,128)(2,1)S(1)} collective-permute-done((bf16[4,8,2,8,128]{4,3,2,1,0:T(8,128)(2,1)S(1)}, bf16[4,8,2,8,128]{4,3,2,1,0:T(8,128)(2,1)S(1)}, u32[]{:S(2)}, u32[]{:S(2)}) %collective-permute-start.5) | collective-permute-done | bytes 131104 | tf_op jit(solution)/shard_map/ppermute | solution.py:446
  16.4 1.4 %collective-permute-done.4.refs_2_ = bf16[4,8,2,8,128]{4,3,2,1,0:T(8,128)(2,1)S(1)} collective-permute-done((bf16[4,8,2,8,128]{4,3,2,1,0:T(8,128)(2,1)S(1)}, bf16[4,8,2,8,128]{4,3,2,1,0:T(8,128)(2,1)S(1)}, u32[]{:S(2)}, u32[]{:S(2)}) %collective-permute-start.4) | collective-permute-done | bytes 131104 | tf_op jit(solution)/shard_map/ppermute | solution.py:441
  17.8 0.4 collective-permute-done.3.refs_1_
  18.2 0.3 copy-done.6
  18.5 0.6 %copy-done.7 = bf16[4,8,2,8,128]{4,3,2,1,0:T(8,128)(2,1)} copy-done((bf16[4,8,2,8,128]{4,3,2,1,0:T(8,128)(2,1)}, bf16[4,8,2,8,128]{4,3,2,1,0:T(8,128)(2,1)S(1)}, u32[]{:S(2)}) %copy-start.7) | copy-done | bytes 131096
  19.1 6.4 %shard_map.82 = (bf16[32,32,128]{2,1,0:T(8,128)(2,1)}, bf16[32,32,128]{2,1,0:T(8,128)(2,1)}) custom-call(bf16[4,8,2,8,128]{4,3,2,1,0:T(8,128)(2,1)} %copy-done.1, bf16[4,8,2,8,128]{4,3,2,1,0:T(8,128)(2,1)} %copy-done.7, bf16[4,8,2,8,128]{4,3,2,1,0:T(8,128)(2,1)} %copy-done.6, bf16[4,8,2,8,128]{4,3,2,1,0:T(8,128)(2,1)} %copy-done.5, ...), custom_call_target="tpu_custom_call" | custom-call | tf_op jit(solution)/shard_map/pallas_call | solution.py:414
  25.5 0.0 collective-permute-start.6
  25.5 1.7 %collective-permute-done.6.recv = bf16[32,32,128]{2,1,0:T(8,128)(2,1)S(1)} collective-permute-done((bf16[32,32,128]{2,1,0:T(8,128)(2,1)}, bf16[32,32,128]{2,1,0:T(8,128)(2,1)S(1)}, u32[]{:S(2)}, u32[]{:S(2)}) %collective-permute-start.6) | collective-permute-done | bytes 262176 | tf_op jit(solution)/shard_map/ppermute | solution.py:449
  27.2 0.7 %copy-done.2 = bf16[32,32,128]{2,1,0:T(8,128)(2,1)} copy-done((bf16[32,32,128]{2,1,0:T(8,128)(2,1)}, bf16[32,32,128]{2,1,0:T(8,128)(2,1)S(1)}, u32[]{:S(2)}) %copy-start.2) | copy-done | bytes 262168
  27.9 6.3 %shard_map.83 = (bf16[32,64,128]{2,1,0:T(8,128)(2,1)}, bf16[32,32,128]{2,1,0:T(8,128)(2,1)}, bf16[32,32,128]{2,1,0:T(8,128)(2,1)}) custom-call(bf16[32,32,128]{2,1,0:T(8,128)(2,1)} %get-tuple-element.12.keep, bf16[32,32,128]{2,1,0:T(8,128)(2,1)} %copy-done.2, bf16[2,2,128,256]{3,2,1,0:T(8,128)(2,1)} %w_key.5, ...), custom_call_target="tpu_custom_call" | custom-call | tf_op jit(solution)/shard_map/pallas_call | solution.py:414
  34.3 0.1 collective-permute-start.7
  34.4 1.6 %collective-permute-done.7.recv = bf16[32,32,128]{2,1,0:T(8,128)(2,1)S(1)} collective-permute-done((bf16[32,32,128]{2,1,0:T(8,128)(2,1)}, bf16[32,32,128]{2,1,0:T(8,128)(2,1)S(1)}, u32[]{:S(2)}, u32[]{:S(2)}) %collective-permute-start.7) | collective-permute-done | bytes 262176 | tf_op jit(solution)/shard_map/ppermute | solution.py:449
  36.0 0.7 %copy-done.3 = bf16[32,32,128]{2,1,0:T(8,128)(2,1)} copy-done((bf16[32,32,128]{2,1,0:T(8,128)(2,1)}, bf16[32,32,128]{2,1,0:T(8,128)(2,1)S(1)}, u32[]{:S(2)}) %copy-start.3) | copy-done | bytes 262168
  36.7 8.9 %shard_map.84 = (bf16[24,32,128]{2,1,0:T(8,128)(2,1)}, bf16[24,32,128]{2,1,0:T(8,128)(2,1)}) custom-call(bf16[32,64,128]{2,1,0:T(8,128)(2,1)} %get-tuple-element.14.slab, bf16[32,32,128]{2,1,0:T(8,128)(2,1)} %get-tuple-element.15.own, bf16[32,32,128]{2,1,0:T(8,128)(2,1)} %copy-done.3, bf16[2,128,512]{2,1,0:T(8,128)(2,1)} %w_in.3, ...), custom_call_target="tpu_custom_call" | custom-call | tf_op jit(solution)/shard_map/pallas_call | solution.py:414
  45.7 0.1 collective-permute-start.8
  45.8 1.5 %collective-permute-done.8.recv = bf16[24,32,128]{2,1,0:T(8,128)(2,1)S(1)} collective-permute-done((bf16[24,32,128]{2,1,0:T(8,128)(2,1)}, bf16[24,32,128]{2,1,0:T(8,128)(2,1)S(1)}, u32[]{:S(2)}, u32[]{:S(2)}) %collective-permute-start.8) | collective-permute-done | bytes 196640 | tf_op jit(solution)/shard_map/ppermute | solution.py:449
  47.3 0.7 %copy-done.4 = bf16[24,32,128]{2,1,0:T(8,128)(2,1)} copy-done((bf16[24,32,128]{2,1,0:T(8,128)(2,1)}, bf16[24,32,128]{2,1,0:T(8,128)(2,1)S(1)}, u32[]{:S(2)}) %copy-start.4) | copy-done | bytes 196632
  48.0 4.6 %shard_map.85 = bf16[8,1,2,8,128]{4,3,2,1,0:T(8,128)(2,1)} custom-call(bf16[24,32,128]{2,1,0:T(8,128)(2,1)} %get-tuple-element.17.keep, bf16[24,32,128]{2,1,0:T(8,128)(2,1)} %copy-done.4, bf16[2,2,128,256]{3,2,1,0:T(8,128)(2,1)} %w_query.1, bf16[2,2,128,256]{3,2,1,0:T(8,128)(2,1)} %w_key.5, bf16[2,2,128,256]{3,2,1,0:T(8,128)(2,1)} %w_value.1, ...), custom_call_target="tpu_custom_call" | custom-call | tf_op jit(solution)/shard_map/pallas_call | solution.py:414
  (13 shorter events, 0.0 us)
Async XLA Ops:
  0.0 8.0 %copy-start = (bf16[2,2,128,256]{3,2,1,0:T(8,128)(2,1)S(1)}, bf16[2,2,128,256]{3,2,1,0:T(8,128)(2,1)}, u32[]{:S(2)}) copy-start(bf16[2,2,128,256]{3,2,1,0:T(8,128)(2,1)} %w_gate.1) | copy-start | bytes 786436
  0.0 10.1 %copy-start.8 = (bf16[8,1,2,8,128]{4,3,2,1,0:T(8,128)(2,1)S(1)}, bf16[8,1,2,8,128]{4,3,2,1,0:T(8,128)(2,1)}, u32[]{:S(2)}) copy-start(bf16[8,1,2,8,128]{4,3,2,1,0:T(8,128)(2,1)} %param.8) | copy-start | bytes 98308
  0.0 8.2 %collective-permute-start.2 = (bf16[8,2,8,128]{3,2,1,0:T(8,128)(2,1)}, bf16[8,2,8,128]{3,2,1,0:T(8,128)(2,1)S(1)}, u32[]{:S(2)}, u32[]{:S(2)}) collective-permute-start(bf16[8,2,8,128]{3,2,1,0:T(8,128)(2,1)} %bitcast.7), channel_id=1, source_target_pairs={{0,6},{1,7},{2,4},{3,5},{4,2},{5,3},{6,0},{7,1},{8,14},{9,15},{10,... | collective-permute-start | bytes 98312 | tf_op jit(solution)/shard_map/ppermute | solution.py:439
  5.1 5.0 %collective-permute-start.1 = (bf16[8,2,8,128]{3,2,1,0:T(8,128)(2,1)}, bf16[8,2,8,128]{3,2,1,0:T(8,128)(2,1)S(1)}, u32[]{:S(2)}, u32[]{:S(2)}) collective-permute-start(bf16[8,2,8,128]{3,2,1,0:T(8,128)(2,1)} %bitcast.8), channel_id=1, source_target_pairs={{0,4},{1,5},{2,6},{3,7},{4,0},{5,1},{6,2},{7,3},{8,12},{9,13},{10,... | collective-permute-start | bytes 98312 | tf_op jit(solution)/shard_map/ppermute | solution.py:439
  5.1 5.0 %collective-permute-start = (bf16[8,2,8,128]{3,2,1,0:T(8,128)(2,1)}, bf16[8,2,8,128]{3,2,1,0:T(8,128)(2,1)S(1)}, u32[]{:S(2)}, u32[]{:S(2)}) collective-permute-start(bf16[8,2,8,128]{3,2,1,0:T(8,128)(2,1)} %bitcast.9), channel_id=1, source_target_pairs={{0,2},{1,3},{2,0},{3,1},{4,6},{5,7},{6,4},{7,5},{8,10},{9,11},{10,... | collective-permute-start | bytes 98312 | tf_op jit(solution)/shard_map/ppermute | solution.py:439
  10.1 4.5 %copy-start.1 = (bf16[4,8,2,8,128]{4,3,2,1,0:T(8,128)(2,1)}, bf16[4,8,2,8,128]{4,3,2,1,0:T(8,128)(2,1)S(1)}, u32[]{:S(2)}) copy-start(bf16[4,8,2,8,128]{4,3,2,1,0:T(8,128)(2,1)S(1)} %pad_maximum_fusion.refs_0_) | copy-start | bytes 393220
  10.1 6.3 %collective-permute-start.5 = (bf16[4,8,2,8,128]{4,3,2,1,0:T(8,128)(2,1)S(1)}, bf16[4,8,2,8,128]{4,3,2,1,0:T(8,128)(2,1)S(1)}, u32[]{:S(2)}, u32[]{:S(2)}) collective-permute-start(bf16[4,8,2,8,128]{4,3,2,1,0:T(8,128)(2,1)S(1)} %pad_maximum_fusion.refs_0_), channel_id=1, source_target_pairs={{0,17},{1,16},{2,19},{3,18},{4,21},{5,20},{6,23},{7,22},{8,25},{9,... | collective-permute-start | bytes 393224 | tf_op jit(solution)/shard_map/ppermute | solution.py:446
  12.7 5.1 %collective-permute-start.4 = (bf16[4,8,2,8,128]{4,3,2,1,0:T(8,128)(2,1)S(1)}, bf16[4,8,2,8,128]{4,3,2,1,0:T(8,128)(2,1)S(1)}, u32[]{:S(2)}, u32[]{:S(2)}) collective-permute-start(bf16[4,8,2,8,128]{4,3,2,1,0:T(8,128)(2,1)S(1)} %pad_maximum_fusion.refs_0_), channel_id=1, source_target_pairs={{0,16},{8,24},{16,0},{24,8},{1,17},{9,25},{17,1},{25,9},{2,18},{10... | collective-permute-start | bytes 393224 | tf_op jit(solution)/shard_map/ppermute | solution.py:441
  13.2 5.0 %collective-permute-start.3 = (bf16[4,8,2,8,128]{4,3,2,1,0:T(8,128)(2,1)S(1)}, bf16[4,8,2,8,128]{4,3,2,1,0:T(8,128)(2,1)S(1)}, u32[]{:S(2)}, u32[]{:S(2)}) collective-permute-start(bf16[4,8,2,8,128]{4,3,2,1,0:T(8,128)(2,1)S(1)} %pad_maximum_fusion.refs_0_), channel_id=1, source_target_pairs={{0,1},{1,0},{2,3},{3,2},{4,5},{5,4},{6,7},{7,6},{8,9},{9,8},{10,11... | collective-permute-start | bytes 393224 | tf_op jit(solution)/shard_map/ppermute | solution.py:439
  16.4 1.7 %copy-start.5 = (bf16[4,8,2,8,128]{4,3,2,1,0:T(8,128)(2,1)}, bf16[4,8,2,8,128]{4,3,2,1,0:T(8,128)(2,1)S(1)}, u32[]{:S(2)}) copy-start(bf16[4,8,2,8,128]{4,3,2,1,0:T(8,128)(2,1)S(1)} %collective-permute-done.5.refs_3_) | copy-start | bytes 393220
  17.8 0.7 %copy-start.6 = (bf16[4,8,2,8,128]{4,3,2,1,0:T(8,128)(2,1)}, bf16[4,8,2,8,128]{4,3,2,1,0:T(8,128)(2,1)S(1)}, u32[]{:S(2)}) copy-start(bf16[4,8,2,8,128]{4,3,2,1,0:T(8,128)(2,1)S(1)} %collective-permute-done.4.refs_2_) | copy-start | bytes 393220
  18.5 0.6 %copy-start.7 = (bf16[4,8,2,8,128]{4,3,2,1,0:T(8,128)(2,1)}, bf16[4,8,2,8,128]{4,3,2,1,0:T(8,128)(2,1)S(1)}, u32[]{:S(2)}) copy-start(bf16[4,8,2,8,128]{4,3,2,1,0:T(8,128)(2,1)S(1)} %collective-permute-done.3.refs_1_) | copy-start | bytes 393220
  25.5 1.7 %collective-permute-start.6 = (bf16[32,32,128]{2,1,0:T(8,128)(2,1)}, bf16[32,32,128]{2,1,0:T(8,128)(2,1)S(1)}, u32[]{:S(2)}, u32[]{:S(2)}) collective-permute-start(bf16[32,32,128]{2,1,0:T(8,128)(2,1)} %get-tuple-element.13), channel_id=1, source_target_pairs={{0,8},{8,0},{16,24},{24,16},{1,9},{9,1},{17,25},{25,17},{2,10},{10... | collective-permute-start | bytes 786440 | tf_op jit(solution)/shard_map/ppermute | solution.py:449
  27.2 0.7 %copy-start.2 = (bf16[32,32,128]{2,1,0:T(8,128)(2,1)}, bf16[32,32,128]{2,1,0:T(8,128)(2,1)S(1)}, u32[]{:S(2)}) copy-start(bf16[32,32,128]{2,1,0:T(8,128)(2,1)S(1)} %collective-permute-done.6.recv) | copy-start | bytes 786436
  34.3 1.7 %collective-permute-start.7 = (bf16[32,32,128]{2,1,0:T(8,128)(2,1)}, bf16[32,32,128]{2,1,0:T(8,128)(2,1)S(1)}, u32[]{:S(2)}, u32[]{:S(2)}) collective-permute-start(bf16[32,32,128]{2,1,0:T(8,128)(2,1)} %get-tuple-element.16), channel_id=1, source_target_pairs={{0,8},{8,0},{16,24},{24,16},{1,9},{9,1},{17,25},{25,17},{2,10},{10... | collective-permute-start | bytes 786440 | tf_op jit(solution)/shard_map/ppermute | solution.py:449
  36.0 0.7 %copy-start.3 = (bf16[32,32,128]{2,1,0:T(8,128)(2,1)}, bf16[32,32,128]{2,1,0:T(8,128)(2,1)S(1)}, u32[]{:S(2)}) copy-start(bf16[32,32,128]{2,1,0:T(8,128)(2,1)S(1)} %collective-permute-done.7.recv) | copy-start | bytes 786436
  45.7 1.7 %collective-permute-start.8 = (bf16[24,32,128]{2,1,0:T(8,128)(2,1)}, bf16[24,32,128]{2,1,0:T(8,128)(2,1)S(1)}, u32[]{:S(2)}, u32[]{:S(2)}) collective-permute-start(bf16[24,32,128]{2,1,0:T(8,128)(2,1)} %get-tuple-element.18), channel_id=1, source_target_pairs={{0,8},{8,0},{16,24},{24,16},{1,9},{9,1},{17,25},{25,17},{2,10},{10... | collective-permute-start | bytes 589832 | tf_op jit(solution)/shard_map/ppermute | solution.py:449
  47.3 0.7 %copy-start.4 = (bf16[24,32,128]{2,1,0:T(8,128)(2,1)}, bf16[24,32,128]{2,1,0:T(8,128)(2,1)S(1)}, u32[]{:S(2)}) copy-start(bf16[24,32,128]{2,1,0:T(8,128)(2,1)S(1)} %collective-permute-done.8.recv) | copy-start | bytes 589828

commit v3 on v2

--- a/solution.py
+++ b/solution.py
@@ -13,6 +13,7 @@
 LANES = 128
 SUBLANES = 8
 VMEM_BUDGET = 24 * 2**20
+VMEM_GRANT = 36 * 2**20
 
 
 epsilon = 1e-05
@@ -418,6 +419,7 @@
         out_specs=[whole(shape) for shape in outs],
         out_shape=[jax.ShapeDtypeStruct(shape, jnp.bfloat16) for shape in outs],
         scratch_shapes=scratch,
+        compiler_params=pltpu.CompilerParams(vmem_limit_bytes=VMEM_GRANT),
     )(*arrays, *[entry[0] for entry in weights])
 
 

time: 52.9 us -> 42.1 us (0.80)
  Pallas kernels: 26.3 us -> 19 us
  local copies, waits for them, and re-layouts: 5.43 us -> 2.44 us
  other arithmetic: 0.95 us -> 0.07 us
    pallas_call x4, Pallas kernels: 26.3 us -> 19 us  [call(): pl.pallas_call(kernel, grid=(1,), in_specs=[whole(array.shape) for array...]
    unnamed x21 -> x19, local copies, waits for them, and re-layouts: 5.43 us -> 2.44 us
    transpose x1, other arithmetic: 0.93 us -> 0.05 us  [local_gathered(): jnp.swapaxes(jnp.concatenate([w_query, w_value, w_gate], axis=3), 2, 3)]
    ppermute x1, waiting for transfers between devices: 1.79 us -> 2.67 us  [moved(): return lax.ppermute(array, ('row', 'col'), routes)]
    ppermute x3, waiting for transfers between devices: 4.87 us -> 4.23 us  [to_partner(): return lax.ppermute(array, 'row', [(r, r ^ 1) for r in range(row_count)])]
where the time goes in v3:
time: 42.1 us; the launch traced here: 42 us
  Pallas kernels  19 us (45%)
  waiting for transfers between devices  10.6 us (25%)
  starting transfers between devices  9.74 us (23%)
  local copies, waits for them, and re-layouts  2.44 us (6%)
    pallas_call x4, Pallas kernels, call(): pl.pallas_call(kernel, grid=(1,), in_specs=[whole(array.shape) for array...  19 us
    ppermute x4, starting transfers between devices, moved(): return lax.ppermute(array, 'col', [(c, c ^ dc) for c in range(col_count)])  6.22 us
    ppermute x3, waiting for transfers between devices, to_partner(): return lax.ppermute(array, 'row', [(r, r ^ 1) for r in range(row_count)])  4.23 us
    ppermute x1, waiting for transfers between devices, moved(): return lax.ppermute(array, ('row', 'col'), routes)  2.67 us
    ppermute x1, starting transfers between devices, moved(): return lax.ppermute(array, ('row', 'col'), routes)  2.51 us
    unnamed x19, local copies, waits for them, and re-layouts  2.44 us
    ppermute x4, waiting for transfers between devices, moved(): return lax.ppermute(array, 'col', [(c, c ^ dc) for c in range(col_count)])  2.32 us
    ppermute x1, waiting for transfers between devices, moved(): lax.ppermute(array, 'row', [(r, r ^ 2 * dx) for r in range(row_count)])  1.36 us
  transfers between devices with their start and end apart: 9, of which 7 were waited for; matrix products, arithmetic and copies ran while one was open for 6% of the time, Pallas kernels for 0%

profile of v3, /device:TPU:0, one launch (start us, length us, event | category | flops | bytes accessed | tf_op | source)
XLA Modules:
  0.0 42.0 jit_solution(8875075524476030121)
XLA Ops:
  0.0 5.1 %collective-permute-start.2 = (bf16[8,2,8,128]{3,2,1,0:T(8,128)(2,1)}, bf16[8,2,8,128]{3,2,1,0:T(8,128)(2,1)S(1)}, u32[]{:S(2)}, u32[]{:S(2)}) collective-permute-start(bf16[8,2,8,128]{3,2,1,0:T(8,128)(2,1)} %bitcast.7), channel_id=1, source_target_pairs={{0,6},{1,7},{2,4},{3,5},{4,2},{5,3},{6,0},{7,1},{8,14},{9,15},{10,... | collective-permute-start | bytes 98312 | tf_op jit(solution)/shard_map/ppermute | solution.py:441
  5.1 0.0 collective-permute-start.1
  5.1 0.6 %collective-permute-start = (bf16[8,2,8,128]{3,2,1,0:T(8,128)(2,1)}, bf16[8,2,8,128]{3,2,1,0:T(8,128)(2,1)S(1)}, u32[]{:S(2)}, u32[]{:S(2)}) collective-permute-start(bf16[8,2,8,128]{3,2,1,0:T(8,128)(2,1)} %bitcast.9), channel_id=1, source_target_pairs={{0,2},{1,3},{2,0},{3,1},{4,6},{5,7},{6,4},{7,5},{8,10},{9,11},{10,... | collective-permute-start | bytes 98312 | tf_op jit(solution)/shard_map/ppermute | solution.py:441
  5.7 1.1 %copy.9 = bf16[2,2,128,256]{2,3,1,0:T(8,128)(2,1)S(1)} copy(bf16[2,2,128,256]{3,2,1,0:T(8,128)(2,1)} %w_query.1) | data formatting | bytes 524288 | tf_op args[1]
  6.8 1.1 %copy.10 = bf16[2,2,128,256]{2,3,1,0:T(8,128)(2,1)S(1)} copy(bf16[2,2,128,256]{3,2,1,0:T(8,128)(2,1)} %w_value.1) | data formatting | bytes 524288 | tf_op args[3]
  8.0 0.0 copy-done.2
  8.0 0.2 copy.11
  8.2 0.0 collective-permute-done.2
  8.2 1.9 %collective-permute-done.1 = bf16[8,2,8,128]{3,2,1,0:T(8,128)(2,1)S(1)} collective-permute-done((bf16[8,2,8,128]{3,2,1,0:T(8,128)(2,1)}, bf16[8,2,8,128]{3,2,1,0:T(8,128)(2,1)S(1)}, u32[]{:S(2)}, u32[]{:S(2)}) %collective-permute-start.1) | collective-permute-done | bytes 32800 | tf_op jit(solution)/shard_map/ppermute | solution.py:441
  10.1 0.0 collective-permute-done
  10.1 0.0 copy-done.7
  10.1 0.0 copy-start
  10.1 0.0 copy-start.1
  10.2 2.5 %collective-permute-start.5 = (bf16[4,8,2,8,128]{4,3,2,1,0:T(8,128)(2,1)S(1)}, bf16[4,8,2,8,128]{4,3,2,1,0:T(8,128)(2,1)S(1)}, u32[]{:S(2)}, u32[]{:S(2)}) collective-permute-start(bf16[4,8,2,8,128]{4,3,2,1,0:T(8,128)(2,1)S(1)} %pad_maximum_fusion.refs_0_), channel_id=1, source_target_pairs={{0,17},{1,16},{2,19},{3,18},{4,21},{5,20},{6,23},{7,22},{8,25},{9,... | collective-permute-start | bytes 393224 | tf_op jit(solution)/shard_map/ppermute | solution.py:448
  12.7 0.5 %collective-permute-start.4 = (bf16[4,8,2,8,128]{4,3,2,1,0:T(8,128)(2,1)S(1)}, bf16[4,8,2,8,128]{4,3,2,1,0:T(8,128)(2,1)S(1)}, u32[]{:S(2)}, u32[]{:S(2)}) collective-permute-start(bf16[4,8,2,8,128]{4,3,2,1,0:T(8,128)(2,1)S(1)} %pad_maximum_fusion.refs_0_), channel_id=1, source_target_pairs={{0,16},{8,24},{16,0},{24,8},{1,17},{9,25},{17,1},{25,9},{2,18},{10... | collective-permute-start | bytes 393224 | tf_op jit(solution)/shard_map/ppermute | solution.py:443
  13.2 0.5 %collective-permute-start.3 = (bf16[4,8,2,8,128]{4,3,2,1,0:T(8,128)(2,1)S(1)}, bf16[4,8,2,8,128]{4,3,2,1,0:T(8,128)(2,1)S(1)}, u32[]{:S(2)}, u32[]{:S(2)}) collective-permute-start(bf16[4,8,2,8,128]{4,3,2,1,0:T(8,128)(2,1)S(1)} %pad_maximum_fusion.refs_0_), channel_id=1, source_target_pairs={{0,1},{1,0},{2,3},{3,2},{4,5},{5,4},{6,7},{7,6},{8,9},{9,8},{10,11... | collective-permute-start | bytes 393224 | tf_op jit(solution)/shard_map/ppermute | solution.py:441
  13.7 0.1 maximum_bitcast_fusion.refs_5_.w_rest
  13.8 2.7 %collective-permute-done.5.refs_3_ = bf16[4,8,2,8,128]{4,3,2,1,0:T(8,128)(2,1)S(1)} collective-permute-done((bf16[4,8,2,8,128]{4,3,2,1,0:T(8,128)(2,1)S(1)}, bf16[4,8,2,8,128]{4,3,2,1,0:T(8,128)(2,1)S(1)}, u32[]{:S(2)}, u32[]{:S(2)}) %collective-permute-start.5) | collective-permute-done | bytes 131104 | tf_op jit(solution)/shard_map/ppermute | solution.py:448
  16.4 1.4 %collective-permute-done.4.refs_2_ = bf16[4,8,2,8,128]{4,3,2,1,0:T(8,128)(2,1)S(1)} collective-permute-done((bf16[4,8,2,8,128]{4,3,2,1,0:T(8,128)(2,1)S(1)}, bf16[4,8,2,8,128]{4,3,2,1,0:T(8,128)(2,1)S(1)}, u32[]{:S(2)}, u32[]{:S(2)}) %collective-permute-start.4) | collective-permute-done | bytes 131104 | tf_op jit(solution)/shard_map/ppermute | solution.py:443
  17.8 0.4 collective-permute-done.3.refs_1_
  18.2 0.0 copy-done.1
  18.2 4.5 %shard_map.82 = (bf16[32,32,128]{2,1,0:T(8,128)(2,1)S(1)}, bf16[32,32,128]{2,1,0:T(8,128)(2,1)S(1)}) custom-call(bf16[4,8,2,8,128]{4,3,2,1,0:T(8,128)(2,1)S(1)} %pad_maximum_fusion.refs_0_, bf16[4,8,2,8,128]{4,3,2,1,0:T(8,128)(2,1)S(1)} %collective-permute-done.3.refs_1_, bf16[4,8,2,8,128]{4,3,2,1,0:T(8,128)(2,1)S(1)} %collective-permute-done.4.refs_2_, ...), custom_call_target="tpu_custom_call" | custom-call | tf_op jit(solution)/shard_map/pallas_call | solution.py:415
  22.7 0.1 collective-permute-start.6
  22.8 1.5 %collective-permute-done.6.recv = bf16[32,32,128]{2,1,0:T(8,128)(2,1)S(1)} collective-permute-done((bf16[32,32,128]{2,1,0:T(8,128)(2,1)S(1)}, bf16[32,32,128]{2,1,0:T(8,128)(2,1)S(1)}, u32[]{:S(2)}, u32[]{:S(2)}) %collective-permute-start.6) | collective-permute-done | bytes 262176 | tf_op jit(solution)/shard_map/ppermute | solution.py:451
  24.3 4.3 %shard_map.83 = (bf16[32,64,128]{2,1,0:T(8,128)(2,1)S(1)}, bf16[32,32,128]{2,1,0:T(8,128)(2,1)S(1)}, bf16[32,32,128]{2,1,0:T(8,128)(2,1)S(1)}) custom-call(bf16[32,32,128]{2,1,0:T(8,128)(2,1)S(1)} %get-tuple-element.12.keep, bf16[32,32,128]{2,1,0:T(8,128)(2,1)S(1)} %collective-permute-done.6.recv, bf16[2,2,128,256]{3,2,1,0:T(8,128)(2,1)S(1)} %copy-done, ...), custom_call_target="tpu_custom_call" | custom-call | tf_op jit(solution)/shard_map/pallas_call | solution.py:415
  28.6 0.2 collective-permute-start.7
  28.8 1.4 %collective-permute-done.7.recv = bf16[32,32,128]{2,1,0:T(8,128)(2,1)S(1)} collective-permute-done((bf16[32,32,128]{2,1,0:T(8,128)(2,1)S(1)}, bf16[32,32,128]{2,1,0:T(8,128)(2,1)S(1)}, u32[]{:S(2)}, u32[]{:S(2)}) %collective-permute-start.7) | collective-permute-done | bytes 262176 | tf_op jit(solution)/shard_map/ppermute | solution.py:451
  30.2 0.0 copy-done.6
  30.2 6.9 %shard_map.84 = (bf16[24,32,128]{2,1,0:T(8,128)(2,1)S(1)}, bf16[24,32,128]{2,1,0:T(8,128)(2,1)S(1)}) custom-call(bf16[32,64,128]{2,1,0:T(8,128)(2,1)S(1)} %get-tuple-element.14.slab, bf16[32,32,128]{2,1,0:T(8,128)(2,1)S(1)} %get-tuple-element.15.own, bf16[32,32,128]{2,1,0:T(8,128)(2,1)S(1)} %collective-permute-done.7.recv, ...), custom_call_target="tpu_custom_call" | custom-call | tf_op jit(solution)/shard_map/pallas_call | solution.py:415
  37.1 0.2 collective-permute-start.8
  37.3 1.3 %collective-permute-done.8.recv = bf16[24,32,128]{2,1,0:T(8,128)(2,1)S(1)} collective-permute-done((bf16[24,32,128]{2,1,0:T(8,128)(2,1)S(1)}, bf16[24,32,128]{2,1,0:T(8,128)(2,1)S(1)}, u32[]{:S(2)}, u32[]{:S(2)}) %collective-permute-start.8) | collective-permute-done | bytes 196640 | tf_op jit(solution)/shard_map/ppermute | solution.py:451
  38.6 3.3 %shard_map.85 = bf16[8,1,2,8,128]{4,3,2,1,0:T(8,128)(2,1)} custom-call(bf16[24,32,128]{2,1,0:T(8,128)(2,1)S(1)} %get-tuple-element.17.keep, bf16[24,32,128]{2,1,0:T(8,128)(2,1)S(1)} %collective-permute-done.8.recv, bf16[2,2,128,256]{3,2,1,0:T(8,128)(2,1)S(1)} %copy-done.4, bf16[2,2,128,256]{3,2,1,0:T(8,128)(2,1)S(1)} %copy-done, ...), custom_call_target="tpu_custom_call" | custom-call | tf_op jit(solution)/shard_map/pallas_call | solution.py:415
  (11 shorter events, 0.0 us)
Async XLA Ops:
  0.0 8.0 %copy-start.2 = (bf16[2,2,128,256]{3,2,1,0:T(8,128)(2,1)S(1)}, bf16[2,2,128,256]{3,2,1,0:T(8,128)(2,1)}, u32[]{:S(2)}) copy-start(bf16[2,2,128,256]{3,2,1,0:T(8,128)(2,1)} %w_gate.1) | copy-start | bytes 786436
  0.0 10.1 %copy-start.7 = (bf16[8,1,2,8,128]{4,3,2,1,0:T(8,128)(2,1)S(1)}, bf16[8,1,2,8,128]{4,3,2,1,0:T(8,128)(2,1)}, u32[]{:S(2)}) copy-start(bf16[8,1,2,8,128]{4,3,2,1,0:T(8,128)(2,1)} %param.8) | copy-start | bytes 98308
  0.0 8.2 %collective-permute-start.2 = (bf16[8,2,8,128]{3,2,1,0:T(8,128)(2,1)}, bf16[8,2,8,128]{3,2,1,0:T(8,128)(2,1)S(1)}, u32[]{:S(2)}, u32[]{:S(2)}) collective-permute-start(bf16[8,2,8,128]{3,2,1,0:T(8,128)(2,1)} %bitcast.7), channel_id=1, source_target_pairs={{0,6},{1,7},{2,4},{3,5},{4,2},{5,3},{6,0},{7,1},{8,14},{9,15},{10,... | collective-permute-start | bytes 98312 | tf_op jit(solution)/shard_map/ppermute | solution.py:441
  5.1 5.0 %collective-permute-start.1 = (bf16[8,2,8,128]{3,2,1,0:T(8,128)(2,1)}, bf16[8,2,8,128]{3,2,1,0:T(8,128)(2,1)S(1)}, u32[]{:S(2)}, u32[]{:S(2)}) collective-permute-start(bf16[8,2,8,128]{3,2,1,0:T(8,128)(2,1)} %bitcast.8), channel_id=1, source_target_pairs={{0,4},{1,5},{2,6},{3,7},{4,0},{5,1},{6,2},{7,3},{8,12},{9,13},{10,... | collective-permute-start | bytes 98312 | tf_op jit(solution)/shard_map/ppermute | solution.py:441
  5.1 5.0 %collective-permute-start = (bf16[8,2,8,128]{3,2,1,0:T(8,128)(2,1)}, bf16[8,2,8,128]{3,2,1,0:T(8,128)(2,1)S(1)}, u32[]{:S(2)}, u32[]{:S(2)}) collective-permute-start(bf16[8,2,8,128]{3,2,1,0:T(8,128)(2,1)} %bitcast.9), channel_id=1, source_target_pairs={{0,2},{1,3},{2,0},{3,1},{4,6},{5,7},{6,4},{7,5},{8,10},{9,11},{10,... | collective-permute-start | bytes 98312 | tf_op jit(solution)/shard_map/ppermute | solution.py:441
  10.1 8.0 %copy-start = (bf16[2,2,128,256]{3,2,1,0:T(8,128)(2,1)S(1)}, bf16[2,2,128,256]{3,2,1,0:T(8,128)(2,1)}, u32[]{:S(2)}) copy-start(bf16[2,2,128,256]{3,2,1,0:T(8,128)(2,1)} %w_key.5) | copy-start | bytes 786436
  10.1 8.0 %copy-start.1 = (bf16[2,2,256,128]{3,2,1,0:T(8,128)(2,1)S(1)}, bf16[2,2,256,128]{3,2,1,0:T(8,128)(2,1)}, u32[]{:S(2)}) copy-start(bf16[2,2,256,128]{3,2,1,0:T(8,128)(2,1)} %w_out.5) | copy-start | bytes 786436
  10.2 6.3 %collective-permute-start.5 = (bf16[4,8,2,8,128]{4,3,2,1,0:T(8,128)(2,1)S(1)}, bf16[4,8,2,8,128]{4,3,2,1,0:T(8,128)(2,1)S(1)}, u32[]{:S(2)}, u32[]{:S(2)}) collective-permute-start(bf16[4,8,2,8,128]{4,3,2,1,0:T(8,128)(2,1)S(1)} %pad_maximum_fusion.refs_0_), channel_id=1, source_target_pairs={{0,17},{1,16},{2,19},{3,18},{4,21},{5,20},{6,23},{7,22},{8,25},{9,... | collective-permute-start | bytes 393224 | tf_op jit(solution)/shard_map/ppermute | solution.py:448
  12.7 5.1 %collective-permute-start.4 = (bf16[4,8,2,8,128]{4,3,2,1,0:T(8,128)(2,1)S(1)}, bf16[4,8,2,8,128]{4,3,2,1,0:T(8,128)(2,1)S(1)}, u32[]{:S(2)}, u32[]{:S(2)}) collective-permute-start(bf16[4,8,2,8,128]{4,3,2,1,0:T(8,128)(2,1)S(1)} %pad_maximum_fusion.refs_0_), channel_id=1, source_target_pairs={{0,16},{8,24},{16,0},{24,8},{1,17},{9,25},{17,1},{25,9},{2,18},{10... | collective-permute-start | bytes 393224 | tf_op jit(solution)/shard_map/ppermute | solution.py:443
  13.2 5.0 %collective-permute-start.3 = (bf16[4,8,2,8,128]{4,3,2,1,0:T(8,128)(2,1)S(1)}, bf16[4,8,2,8,128]{4,3,2,1,0:T(8,128)(2,1)S(1)}, u32[]{:S(2)}, u32[]{:S(2)}) collective-permute-start(bf16[4,8,2,8,128]{4,3,2,1,0:T(8,128)(2,1)S(1)} %pad_maximum_fusion.refs_0_), channel_id=1, source_target_pairs={{0,1},{1,0},{2,3},{3,2},{4,5},{5,4},{6,7},{7,6},{8,9},{9,8},{10,11... | collective-permute-start | bytes 393224 | tf_op jit(solution)/shard_map/ppermute | solution.py:441
  22.7 1.6 %collective-permute-start.6 = (bf16[32,32,128]{2,1,0:T(8,128)(2,1)S(1)}, bf16[32,32,128]{2,1,0:T(8,128)(2,1)S(1)}, u32[]{:S(2)}, u32[]{:S(2)}) collective-permute-start(bf16[32,32,128]{2,1,0:T(8,128)(2,1)S(1)} %get-tuple-element.13), channel_id=1, source_target_pairs={{0,8},{8,0},{16,24},{24,16},{1,9},{9,1},{17,25},{25,17},{2,10},{10... | collective-permute-start | bytes 786440 | tf_op jit(solution)/shard_map/ppermute | solution.py:451
  24.3 5.9 %copy-start.5 = (bf16[2,128,512]{2,1,0:T(8,128)(2,1)S(1)}, bf16[2,128,512]{2,1,0:T(8,128)(2,1)}, u32[]{:S(2)}) copy-start(bf16[2,128,512]{2,1,0:T(8,128)(2,1)} %w_in.3) | copy-start | bytes 786436
  24.3 5.9 %copy-start.6 = (bf16[2,512,128]{2,1,0:T(8,128)(2,1)S(1)}, bf16[2,512,128]{2,1,0:T(8,128)(2,1)}, u32[]{:S(2)}) copy-start(bf16[2,512,128]{2,1,0:T(8,128)(2,1)} %w_back.3) | copy-start | bytes 786436
  28.6 1.6 %collective-permute-start.7 = (bf16[32,32,128]{2,1,0:T(8,128)(2,1)S(1)}, bf16[32,32,128]{2,1,0:T(8,128)(2,1)S(1)}, u32[]{:S(2)}, u32[]{:S(2)}) collective-permute-start(bf16[32,32,128]{2,1,0:T(8,128)(2,1)S(1)} %get-tuple-element.16), channel_id=1, source_target_pairs={{0,8},{8,0},{16,24},{24,16},{1,9},{9,1},{17,25},{25,17},{2,10},{10... | collective-permute-start | bytes 786440 | tf_op jit(solution)/shard_map/ppermute | solution.py:451
  30.2 8.4 %copy-start.3 = (bf16[2,2,128,256]{3,2,1,0:T(8,128)(2,1)S(1)}, bf16[2,2,128,256]{3,2,1,0:T(8,128)(2,1)}, u32[]{:S(2)}) copy-start(bf16[2,2,128,256]{3,2,1,0:T(8,128)(2,1)} %w_value.1) | copy-start | bytes 786436
  30.2 8.4 %copy-start.4 = (bf16[2,2,128,256]{3,2,1,0:T(8,128)(2,1)S(1)}, bf16[2,2,128,256]{3,2,1,0:T(8,128)(2,1)}, u32[]{:S(2)}) copy-start(bf16[2,2,128,256]{3,2,1,0:T(8,128)(2,1)} %w_query.1) | copy-start | bytes 786436
  37.1 1.5 %collective-permute-start.8 = (bf16[24,32,128]{2,1,0:T(8,128)(2,1)S(1)}, bf16[24,32,128]{2,1,0:T(8,128)(2,1)S(1)}, u32[]{:S(2)}, u32[]{:S(2)}) collective-permute-start(bf16[24,32,128]{2,1,0:T(8,128)(2,1)S(1)} %get-tuple-element.18), channel_id=1, source_target_pairs={{0,8},{8,0},{16,24},{24,16},{1,9},{9,1},{17,25},{25,17},{2,10},{10... | collective-permute-start | bytes 589832 | tf_op jit(solution)/shard_map/ppermute | solution.py:451
